TPU v7x, 512 devices: a whole 4x8x8 slice. The times are simulated.
512 devices in a mesh: dp: 8 (over x, y_lo), ctx: 64 (over z, y_hi, core).
Axes of the slice: x: 4, y: 8 (y_hi: 4, y_lo: 2; y = y_hi * 2 + y_lo), z: 8, core: 2. Of those that a mesh axis runs over, the one named last changes fastest.
Arguments:
- query_nope: bfloat16 [1536, 128, 128], P('dp', 'ctx'), may hold values from -6 to 6
- query_rope: bfloat16 [1536, 128, 64], P('dp', 'ctx'), may hold values from -8 to 8
- grad_output: bfloat16 [1536, 128, 128], P('dp', 'ctx'), may hold values from -6 to 6
- latents: bfloat16 [1536, 512], P('dp'), may hold values from -6 to 6
- key_rope: bfloat16 [1536, 64], P('dp'), may hold values from -8 to 8
- key_up: bfloat16 [128, 128, 512], P('ctx'), may hold values from -0.25 to 0.25
- value_up: bfloat16 [128, 128, 512], P('ctx'), may hold values from -0.25 to 0.25
- pair_order: int32 [256], replicated, may hold values from 0 to 255, each once
Outputs:
- grad_query_nope: bfloat16 [1536, 128, 128], P('dp', 'ctx')
- grad_query_rope: bfloat16 [1536, 128, 64], P('dp', 'ctx')
- grad_latents: bfloat16 [1536, 512], P(('dp', 'ctx'))
- grad_key_rope: bfloat16 [1536, 64], P(('dp', 'ctx'))
- grad_key_up: float32 [128, 128, 512], P('ctx')
- grad_value_up: float32 [128, 128, 512], P('ctx')
Inputs may be any that keep to these rules, and one draw needn't show every extreme that they name: pair_order holds every number of 0 to 255 once.
All inputs are finite; a program needn't handle non-finite values.
Results may differ from a plain program's by a relative error of at most 0.024.
Values may be sent and summed in bfloat16 or wider, within the bound.
A program may use at most 64 MiB of HBM per device.

v0:
```python
import math

import jax
import jax.numpy as jnp
from jax import lax
from jax.sharding import PartitionSpec as P


def token_positions(order_row, dev_count, tok_dev):
    pair_count = order_row.shape[0]
    per_dev = pair_count // dev_count
    group_len = tok_dev // (2 * per_dev)
    half_len = tok_dev // 2
    within = jnp.arange(tok_dev, dtype=jnp.int32)
    slot_ids = within % half_len // group_len
    pair_ids = order_row.reshape(dev_count, per_dev)[:, slot_ids]
    late_ids = 2 * pair_count - 1 - pair_ids
    group_ids = jnp.where(within[None, :] < half_len, pair_ids, late_ids)
    return (group_ids * group_len + (within % group_len)[None, :]).reshape(-1)


def attend_local(
    absorbed, query_part, grad_lat_out, all_latents, all_krope, query_pos, key_pos, softmax_scale
):
    scores = (
        jnp.einsum("qhl,ul->qhu", absorbed, all_latents, preferred_element_type=jnp.float32)
        + jnp.einsum("qhr,ur->qhu", query_part, all_krope, preferred_element_type=jnp.float32)
    ) * softmax_scale
    allowed = (key_pos[None, :] <= query_pos[:, None])[:, None, :]
    scores = jnp.where(allowed, scores, -jnp.inf)
    row_max = jnp.max(scores, axis=2, keepdims=True)
    exp_scores = jnp.exp(scores - row_max)
    weights = exp_scores / jnp.sum(exp_scores, axis=2, keepdims=True)
    weights_bf = weights.astype(jnp.bfloat16)
    latent_out = jnp.einsum(
        "qhu,ul->qhl", weights_bf, all_latents, preferred_element_type=jnp.float32
    )
    row_dot = jnp.sum(grad_lat_out.astype(jnp.float32) * latent_out, axis=2, keepdims=True)
    grad_weights = jnp.einsum(
        "qhl,ul->qhu", grad_lat_out, all_latents, preferred_element_type=jnp.float32
    )
    grad_scores = (weights * (grad_weights - row_dot) * softmax_scale).astype(jnp.bfloat16)
    grad_absorbed = jnp.einsum(
        "qhu,ul->qhl", grad_scores, all_latents, preferred_element_type=jnp.float32
    ).astype(jnp.bfloat16)
    grad_rope = jnp.einsum(
        "qhu,ur->qhr", grad_scores, all_krope, preferred_element_type=jnp.float32
    ).astype(jnp.bfloat16)
    lat_terms = jnp.einsum(
        "qhu,qhl->ul", grad_scores, absorbed, preferred_element_type=jnp.float32
    ) + jnp.einsum("qhu,qhl->ul", weights_bf, grad_lat_out, preferred_element_type=jnp.float32)
    rope_terms = jnp.einsum(
        "qhu,qhr->ur", grad_scores, query_part, preferred_element_type=jnp.float32
    )
    return (latent_out.astype(jnp.bfloat16), grad_absorbed, grad_rope, lat_terms, rope_terms)


def on_device(query_nope, query_rope, grad_output, latents, key_rope, key_up, value_up, pair_order):
    tok_dev = query_nope.shape[0]
    softmax_scale = 1.0 / math.sqrt(query_nope.shape[2] + query_rope.shape[2])
    all_pos = token_positions(pair_order, lax.axis_size("dp"), tok_dev)
    own_pos = lax.dynamic_slice_in_dim(all_pos, lax.axis_index("dp") * tok_dev, tok_dev, 0)
    all_latents, all_krope = (
        lax.all_gather(latents, "dp", axis=0, tiled=True),
        lax.all_gather(key_rope, "dp", axis=0, tiled=True),
    )
    absorbed = jnp.einsum(
        "shd,hdl->shl", query_nope, key_up, preferred_element_type=jnp.float32
    ).astype(jnp.bfloat16)
    grad_lat_out = jnp.einsum(
        "shv,hvl->shl", grad_output, value_up, preferred_element_type=jnp.float32
    ).astype(jnp.bfloat16)
    head_out, head_gabs, grad_rope, lat_terms, rope_terms = attend_local(
        absorbed, query_rope, grad_lat_out, all_latents, all_krope, own_pos, all_pos, softmax_scale
    )
    grad_nope = jnp.einsum(
        "shl,hdl->shd", head_gabs, key_up, preferred_element_type=jnp.float32
    ).astype(jnp.bfloat16)
    own_lat, own_rope = (
        lax.psum_scatter(lat_terms, ("dp", "ctx"), scatter_dimension=0, tiled=True),
        lax.psum_scatter(rope_terms, ("dp", "ctx"), scatter_dimension=0, tiled=True),
    )
    grad_kup = jnp.einsum("shd,shl->hdl", query_nope, head_gabs, preferred_element_type=jnp.float32)
    grad_vup = jnp.einsum("shv,shl->hvl", grad_output, head_out, preferred_element_type=jnp.float32)
    grad_kup, grad_vup = (
        lax.psum(grad_kup.astype(jnp.bfloat16), "dp").astype(jnp.float32),
        lax.psum(grad_vup.astype(jnp.bfloat16), "dp").astype(jnp.float32),
    )
    return (
        grad_nope,
        grad_rope,
        own_lat.astype(jnp.bfloat16),
        own_rope.astype(jnp.bfloat16),
        grad_kup,
        grad_vup,
    )


def solution(mesh):
    placed = (
        P("dp", "ctx", None),
        P("dp", "ctx", None),
        P("dp", "ctx", None),
        P("dp", None),
        P("dp", None),
        P("ctx", None, None),
        P("ctx", None, None),
        P(),
    )
    return jax.shard_map(
        on_device,
        mesh=mesh,
        in_specs=placed,
        out_specs=(
            P("dp", "ctx", None),
            P("dp", "ctx", None),
            P(("dp", "ctx"), None),
            P(("dp", "ctx"), None),
            P("ctx", None, None),
            P("ctx", None, None),
        ),
        check_vma=False,
    )
```

profile of v0, /device:TPU:1, one launch (start us, length us, event | category | flops | bytes accessed | tf_op | source)
XLA Modules:
  0.0 287.6 jit_solution(7775420926683142371)
XLA Ops:
  7.2 0.0 copy-start
  7.2 0.0 copy-start.12
  7.2 0.0 all-gather.3.cloned.1.call-start
  7.2 0.7 all-gather.3.cloned.1.call-update
  7.9 0.0 all-reduce.7.cloned.1.call-start
  8.0 23.8 %all-gather = bf16[8,192,64]{1,2,0:T(8,128)(2,1)S(1)} all-gather(bf16[1,192,64]{1,2,0:T(8,128)(2,1)} %bitcast.58), channel_id=1, replica_groups=mesh['dp'=8,'ctx'=64] {'dp'}, dimensions={0}, use_global_device_ids=true | all-gather | bytes 221184 | tf_op jit(solution)/shard_map/all_gather | solution.py:65
  31.8 0.1 copy.35
  32.0 0.2 reshape.149
  32.2 0.0 copy-start.5
  32.2 0.1 add.79
  32.3 0.1 broadcast_in_dim.31
  32.4 0.8 reshape.137
  33.2 0.1 copy.32
  33.3 0.7 gather_fusion
  34.0 0.1 copy.33
  34.0 0.1 gather.6
  34.1 0.1 dynamic_slice.3
  34.2 2.0 fusion.19
  36.2 0.0 copy-done
  36.2 0.2 fusion.18
  36.5 0.0 copy-start.2
  36.5 1.9 fusion.34
  38.4 0.2 broadcast_compare_fusion
  38.6 24.6 %all-gather.3.cloned.1.call-done = bf16[1536,512]{1,0:T(8,128)(2,1)} async-done(((bf16[192,512]{1,0:T(8,128)(2,1)}), bf16[1536,512]{1,0:T(8,128)(2,1)}) %all-gather.3.cloned.1.call-update) | async-done | bytes 1572880 | tf_op jit(solution)/shard_map/all_gather | solution.py:64
  63.3 3.1 %fusion.4 = f32[192,2,1536]{2,0,1:T(8,128)S(1)} fusion(f32[192,2,1536]{2,0,1:T(8,128)} %fusion.34, bf16[192,2,512]{2,0,1:T(8,128)(2,1)S(1)} %fusion.18, bf16[1536,512]{1,0:T(8,128)(2,1)} %all-gather.3.cloned.1.call-done, pred[192,1536]{1,0:T(8,128)(4,1)S(1)} %broadcast_compare_fusion), kind=kOutput, calls=%fused_computation.9 | convolution fusion | flops 605749248 | bytes 6979584 | tf_op jit(solution)/shard_map/qhl,ul->qhu/dot_general | solution.py:26
  66.4 0.0 copy-start.8
  66.4 1.9 fusion.33
  68.2 2.9 %convolution_bitcast_fusion = f32[1536,512]{1,0:T(8,128)} fusion(bf16[192,2,512]{2,0,1:T(8,128)(2,1)S(1)} %copy-done.8, f32[192,2]{0,1:T(2,128)S(1)} %get-tuple-element.28, f32[192,2,1536]{2,0,1:T(8,128)S(1)} %fusion.4), kind=kOutput, calls=%fused_computation.3 | convolution fusion | flops 605751168 | bytes 5899776 | tf_op jit(solution)/shard_map/qhu,qhl->ul/dot_general | solution.py:51
  71.1 3.5 %multiply_reduce_fusion = (f32[192,2]{0,1:T(2,128)S(1)}, bf16[192,2,512]{2,0,1:T(8,128)(2,1)}) fusion(bf16[192,2,512]{2,0,1:T(8,128)(2,1)S(1)} %copy-done.8, bf16[1536,512]{1,0:T(8,128)(2,1)} %all-gather.3.cloned.1.call-done, f32[192,2]{0,1:T(2,128)S(1)} %get-tuple-element.28, f32[192,2,1536]{2,0,1:T(8,128)S(1)} %fusion.4), kind=kOutput, calls=%fused_computation.35 | convolution fusion | flops 606537216 | bytes 4721664 | tf_op jit(solution)/shard_map/qhu,ul->qhl/dot_general | solution.py:35
  74.6 3.2 %fusion.8 = bf16[192,2,1536]{2,0,1:T(8,128)(2,1)S(1)} fusion(bf16[192,2,512]{2,0,1:T(8,128)(2,1)S(1)} %copy-done.8, bf16[1536,512]{1,0:T(8,128)(2,1)} %all-gather.3.cloned.1.call-done, f32[192,2]{0,1:T(2,128)S(1)} %get-tuple-element.30, f32[192,2,1536]{2,0,1:T(8,128)} %get-tuple-element.29, f32[192,2]{0,1:T(2,128)S(1)} %get-tuple-element.28), kind=kOutput, calls=%fused_computation.13 | convolution fusion | flops 606928896 | bytes 5508096 | tf_op jit(solution)/shard_map/qhl,ul->qhu/dot_general | solution.py:39
  77.8 1.5 convolution_bitcast_fusion.2
  79.4 1.0 fusion.2
  80.4 0.4 copy-done.7
  80.8 0.8 fusion.15
  81.5 0.0 copy-start.6
  81.6 0.7 copy-done.6
  82.3 1.1 fusion.20
  83.4 1.1 fusion.21
  84.4 115.3 %all-reduce.8 = (bf16[1536,512]{1,0:T(8,128)(2,1)}, bf16[1536,64]{1,0:T(8,128)(2,1)}) all-reduce(f32[1536,512]{1,0:T(8,128)S(1)} %fusion.2, f32[1536,64]{1,0:T(8,128)} %convolution_bitcast_fusion.2), channel_id=2, replica_groups=mesh['dp'=8,'ctx'=64] {'dp','ctx'}, use_global_device_ids=true, to_apply=%region_3.4.clone | all-reduce | flops 884736 | bytes 5308416
  199.7 0.0 all-reduce.7.cloned.1.call-update
  199.7 1.3 fusion.22
  201.0 0.7 copy.39
  201.7 1.3 dynamic-slice_convert_fusion.1
  203.0 1.3 dynamic-slice_convert_fusion
  204.3 2.4 convolution_convert_fusion.5
  206.7 70.3 %all-reduce.7.cloned.1.call-done = (bf16[2,128,512]{1,2,0:T(8,128)(2,1)}, bf16[2,128,512]{1,2,0:T(8,128)(2,1)}) async-done(((bf16[2,128,512]{1,2,0:T(8,128)(2,1)}, bf16[2,128,512]{1,2,0:T(8,128)(2,1)}), (bf16[2,128,512]{1,2,0:T(8,128)(2,1)}, bf16[2,128,512]{1,2,0:T(8,128)(2,1)})) %all-reduce.7.cloned.1.call-update) | async-done | bytes 524304 | tf_op jit(solution)/shard_map/psum | solution.py:86
  277.0 1.9 copy.40
  278.9 1.9 copy.41
  (26 shorter events, 0.1 us)
Async XLA Ops:
  7.2 29.0 %copy-start = (bf16[2,128,512]{2,1,0:T(8,128)(2,1)S(1)}, bf16[2,128,512]{2,1,0:T(8,128)(2,1)}, u32[]{:S(2)}) copy-start(bf16[2,128,512]{2,1,0:T(8,128)(2,1)} %param.13) | copy-start | bytes 786436
  7.2 29.0 %copy-start.10 = (bf16[192,2,128]{2,1,0:T(2,128)(2,1)S(1)}, bf16[192,2,128]{2,1,0:T(2,128)(2,1)}, u32[]{:S(2)}) copy-start(bf16[192,2,128]{2,1,0:T(2,128)(2,1)} %param.8) | copy-start | bytes 294916
  7.2 29.3 %copy-start.12 = (bf16[192,2,64]{0,2,1:T(8,128)(2,1)S(1)}, bf16[192,2,64]{0,2,1:T(8,128)(2,1)}, u32[]{:S(2)}) copy-start(bf16[192,2,64]{0,2,1:T(8,128)(2,1)} %param.9) | copy-start | bytes 147460
  7.2 56.1 %all-gather.3.cloned.1.call-start = ((), (), s32[]{:S(2)}) async-start(), calls=%async_computation | async-start | bytes 1769472 | tf_op jit(solution)/shard_map/all_gather | solution.py:64
  7.9 269.1 %all-reduce.7.cloned.1.call-start = ((), (), s32[]{:S(2)}) async-start(), calls=%async_computation.1 | async-start | bytes 1048576 | tf_op jit(solution)/shard_map/psum | solution.py:86
  32.2 6.5 %copy-start.5 = (bf16[1536,64,1]{0,1,2:T(8,128)(2,1)}, bf16[1536,64,1]{0,1,2:T(8,128)(2,1)S(1)}, u32[]{:S(2)}) copy-start(bf16[1536,64,1]{0,1,2:T(8,128)(2,1)S(1)} %reshape.149) | copy-start | bytes 589828
  36.5 29.9 %copy-start.2 = (bf16[192,2,512]{2,0,1:T(8,128)(2,1)}, bf16[192,2,512]{2,0,1:T(8,128)(2,1)S(1)}, u32[]{:S(2)}) copy-start(bf16[192,2,512]{2,0,1:T(8,128)(2,1)S(1)} %fusion.18) | copy-start | bytes 1179652
  66.4 1.9 copy-start.8
  74.6 3.2 %copy-start.13 = (bf16[192,2,64]{0,2,1:T(8,128)(2,1)S(1)}, bf16[192,2,64]{0,2,1:T(8,128)(2,1)}, u32[]{:S(2)}) copy-start(bf16[192,2,64]{0,2,1:T(8,128)(2,1)} %param.9) | copy-start | bytes 147460
  74.6 4.7 %copy-start.3 = (bf16[192,2,512]{2,0,1:T(8,128)(2,1)S(1)}, bf16[192,2,512]{2,0,1:T(8,128)(2,1)}, u32[]{:S(2)}) copy-start(bf16[192,2,512]{2,0,1:T(8,128)(2,1)} %copy-done.2) | copy-start | bytes 1179652
  74.6 4.7 %copy-start.4 = (f32[1536,512]{1,0:T(8,128)S(1)}, f32[1536,512]{1,0:T(8,128)}, u32[]{:S(2)}) copy-start(f32[1536,512]{1,0:T(8,128)} %convolution_bitcast_fusion) | copy-start | bytes 9437188
  77.8 2.6 copy-start.1
  79.4 1.4 copy-start.7
  80.8 2.6 copy-start.9
  80.8 2.6 copy-start.11
  81.5 0.7 copy-start.6
Sparse Core Ops, SparseCore 0:
  10.1 53.1 all-gather.2
  199.8 77.1 all-reduce.6
where the time goes:
time: 292 us; the launch traced here: 288 us
  blocking collectives  139 us (48%)
  waiting for transfers between devices  95.6 us (33%)
  matrix products  25.9 us (9%)
  between operations  14.3 us (5%)
  local copies, waits for them, and re-layouts  10.5 us (4%)
    unnamed x1, blocking collectives  115 us
    psum x1, waiting for transfers between devices, on_device(): lax.psum(grad_kup.astype(jnp.bfloat16), 'dp').astype(jnp.float32)  70.3 us
    all_gather x1, waiting for transfers between devices, on_device(): lax.all_gather(latents, 'dp', axis=0, tiled=True)  24.6 us
    all_gather x1, blocking collectives, on_device(): lax.all_gather(key_rope, 'dp', axis=0, tiled=True)  23.8 us
    unnamed x32, local copies, waits for them, and re-layouts  5.9 us
  transfers between devices with their start and end apart: 2, of which 2 were waited for; matrix products, arithmetic and copies ran while one was open for 5% of the time, Pallas kernels for 0%

commit v1 on v0

v1 whole, which is shorter than its diff:
```python
import functools
import math

import jax
import jax.numpy as jnp
from jax import lax
from jax.experimental import pallas as pl
from jax.experimental.pallas import tpu as pltpu
from jax.sharding import PartitionSpec as P

MESH = pl.DeviceIdType.MESH
F32 = jnp.float32
BF16 = jnp.bfloat16
NEG = -1e30

NX, NYL, NZ, NYH = 4, 2, 8, 4
TOK = 192
HALF = TOK // 2
DL, DR, DN = 512, 64, 128
ROWS = 2 * TOK
EXT = DL + 2 * DR
PAIRS = 256
PER_DEV = 32
BLK = 4 * HALF + 48
CUT = 224
CH = NZ * 96 + 96
CHH = CH // 2

REL = (0, 3, 1, 2)

N_SEM = 65


def dot(a, b, ca=1, cb=0):
    return lax.dot_general(a, b, (((ca,), (cb,)), ((), ())), preferred_element_type=F32)


def iota(shape, axis):
    return lax.broadcasted_iota(jnp.int32, shape, axis)


def third(v):
    return (v * 43691) >> 17


def kernel(
    q_hbm, qr_hbm, go_hbm, lat_hbm, kr_hbm, kup_hbm, vup_hbm, po_hbm,
    gn_ref, gr_ref, ol_ref, or_ref, gk_ref, gv_ref,
    q_v, qr_v, go_v, kr_v, kup_v, vup_v, po_v,
    agb, lx_s, lxt, ax, axt, gx, gxt, qtx, gotx,
    pcol, prow, st, gw, mb, lb, wt, gst, lot, gat,
    csend, crecv, cown, xs, xsum, r2p, r2m, ra1, ra2, rb1, rb2,
    zs, zrecv, ys, yrecv,
    vb, vry, vs, vr2p, vr2m, vra1, vra2, vrb1, vrb2, vfin,
    vkeep, kb, kr2p, kr2m, kra1, kra2, krb1, krb2, kkeep, kx, kry, kfin,
    lsem, ss, rs,
):
    dp, ctx = lax.axis_index("dp"), lax.axis_index("ctx")
    x, yl = dp // NYL, dp % NYL
    z, yh, c = ctx // (NYH * 2), (ctx // 2) % NYH, ctx % 2
    sib = 1 - c
    xp, xm, x2 = (x + 1) % NX, (x + 3) % NX, (x + 2) % NX

    def device(x_=None, yl_=None, z_=None, yh_=None, c_=None):
        x_, yl_ = x if x_ is None else x_, yl if yl_ is None else yl_
        z_, yh_, c_ = z if z_ is None else z_, yh if yh_ is None else yh_, c if c_ is None else c_
        return {"dp": x_ * NYL + yl_, "ctx": (z_ * NYH + yh_) * 2 + c_}

    to_sib = device(c_=sib)
    to_y = device(yl_=1 - yl)
    to_xp, to_xm = device(x_=xp), device(x_=xm)

    def remote(n, src, dst, dev):
        return pltpu.make_async_remote_copy(
            src_ref=src, dst_ref=dst, send_sem=ss.at[n], recv_sem=rs.at[n],
            device_id=dev, device_id_type=MESH,
        )

    sent = []

    def send(n, src, dst, dev):
        copy = remote(n, src, dst, dev)
        copy.start()
        sent.append(copy)

    def got(n, dst):
        remote(n, dst, dst, to_sib).wait_recv()

    barrier = pltpu.get_barrier_semaphore()

    def greet(dev):
        pl.semaphore_signal(barrier, inc=1, device_id=dev, device_id_type=MESH)

    greet(to_xp)
    greet(to_xm)
    greet(device(yl_=1 - yl))
    for d in range(NYH):
        far = (yh + d) % NYH
        greet(device(yh_=far, c_=sib))
        greet(device(yh_=far, yl_=1 - yl, c_=sib))
        if d:
            greet(device(yh_=far, yl_=(yl + c) % 2, c_=c))
    for d in range(1, NZ):
        greet(device(z_=(z + d) % NZ))

    local = []

    def fetch(src, dst):
        copy = pltpu.make_async_copy(src, dst, lsem.at[len(local)])
        copy.start()
        local.append(copy)
        return copy

    kr_in = fetch(kr_hbm, kr_v)
    lat_in = []
    for h in range(2):
        for t in range(4):
            lat_in.append(fetch(
                lat_hbm.at[pl.ds(h * HALF, HALF), pl.ds(t * 128, 128)],
                agb.at[0, 0, h, pl.ds(t * HALF, HALF)],
            ))
    q_in, kup_in = fetch(q_hbm, q_v), fetch(kup_hbm, kup_v)
    go_in, vup_in = fetch(go_hbm, go_v), fetch(vup_hbm, vup_v)
    qr_in, po_in = fetch(qr_hbm, qr_v), fetch(po_hbm, po_v)

    kr_in.wait()
    kr_own = kr_v[...].astype(F32).T
    krp = jnp.concatenate([kr_own[:HALF], kr_own[HALF:]], axis=1).astype(BF16)
    agb[0, 0, 0, pl.ds(4 * HALF, 48)] = krp[:48]
    agb[0, 0, 1, pl.ds(4 * HALF, 48)] = krp[48:]
    for copy in lat_in:
        copy.wait()

    pl.semaphore_wait(barrier, 21)

    send(0, agb.at[0, 0, c], agb.at[0, 1, c], to_y)
    send(1, agb.at[0, 0, c], agb.at[1, 0, c], to_xp)
    send(2, agb.at[0, 0, c], agb.at[2, 0, c], to_xm)

    q_in.wait()
    go_in.wait()
    kup_in.wait()
    vup_in.wait()
    qr_in.wait()
    po_in.wait()
    blank = jnp.zeros((TOK, DN), F32)

    def block_diagonal(ref):
        top = jnp.concatenate([ref[0].astype(F32), blank], axis=1)
        low = jnp.concatenate([blank, ref[1].astype(F32)], axis=1)
        return jnp.concatenate([top, low], axis=0)

    qx = block_diagonal(q_v)
    gox = block_diagonal(go_v)
    qtx[...] = qx.T.astype(BF16)
    gotx[...] = gox.T.astype(BF16)
    kup2 = kup_v[...].reshape(2 * DN, DL)
    vup2 = vup_v[...].reshape(2 * DN, DL)
    absorbed = dot(qx.astype(BF16), kup2)
    grad_lat = dot(gox.astype(BF16), vup2)
    qr_rows = jnp.concatenate([qr_v[0].astype(F32).T, qr_v[1].astype(F32).T], axis=0)
    qr2 = jnp.concatenate([qr_rows, qr_rows], axis=1)
    ax[:, :DL] = absorbed.astype(BF16)
    ax[:, DL:] = qr2.astype(BF16)
    axt[:DL, :] = absorbed.T.astype(BF16)
    axt[DL:, :] = qr2.T.astype(BF16)
    gx[...] = grad_lat.astype(BF16)
    gxt[...] = grad_lat.T.astype(BF16)

    po_row = jnp.broadcast_to(po_v[...].astype(F32), (8, PAIRS))
    slot_t = third(iota((PAIRS, ROWS), 1) % HALF)
    pick = jnp.where(iota((PAIRS, ROWS), 0) == dp * PER_DEV + slot_t, 1.0, 0.0).astype(BF16)
    pid_row = dot(po_row.astype(BF16), pick)
    within = iota((8, ROWS), 1)
    in_half = within % HALF
    late = (within % TOK) >= HALF
    group = jnp.where(late, 2.0 * PAIRS - 1.0 - pid_row, pid_row)
    prow[...] = group * 3.0 + (in_half - 3 * third(in_half)).astype(F32)

    po_col = jnp.broadcast_to(po_row[:1], (128, PAIRS)).T.astype(BF16)
    half_of = iota((TOK, PER_DEV), 0) % HALF
    expand = jnp.where(third(half_of) == iota((TOK, PER_DEV), 1), 1.0, 0.0).astype(BF16)
    row_no = iota((TOK, 128), 0)
    row_half = row_no % HALF
    for b in range(NX * NYL):
        pid = dot(expand, po_col[b * PER_DEV:(b + 1) * PER_DEV])
        grp = jnp.where(row_no >= HALF, 2.0 * PAIRS - 1.0 - pid, pid)
        pcol[b] = grp * 3.0 + (row_half - 3 * third(row_half)).astype(F32)

    scale = 1.0 / math.sqrt(DN + DR)
    low_lane = iota((HALF, 128), 1) < DR

    def attend(k, j):
        b = 2 * k + j
        key_dev = ((x + REL[k]) % NX) * NYL + (yl + j) % 2
        halves = []
        krp = jnp.concatenate(
            [agb[k, j, 0, pl.ds(4 * HALF, 48)], agb[k, j, 1, pl.ds(4 * HALF, 48)]], axis=0
        )
        zero = jnp.zeros((HALF, 128), BF16)
        for h in range(2):
            tiles = [agb[k, j, h, pl.ds(t * HALF, HALF)] for t in range(4)]
            tiles.append(jnp.where(low_lane, krp, zero) if h == 0 else jnp.where(low_lane, zero, krp))
            halves.append(jnp.concatenate(tiles, axis=1))
        lx = jnp.concatenate(halves, axis=0)
        lx_s[pl.ds(b * TOK, TOK), :] = lx
        s = dot(lx, axt[...]) * scale
        gw[b] = dot(lx[:, :DL], gxt[...])
        key_pos = pcol[key_dev]
        allowed = jnp.concatenate([key_pos] * 3, axis=1) <= prow[0:1]
        s = jnp.where(allowed, s, NEG)
        m = jnp.max(s, axis=0, keepdims=True)
        p = jnp.where(allowed, jnp.exp(s - m), 0.0)
        st[b] = p
        mb[b] = jnp.broadcast_to(m, (8, ROWS))
        lb[b] = jnp.broadcast_to(jnp.sum(p, axis=0, keepdims=True), (8, ROWS))

    def attend_pair(k):
        attend(k, 0)
        attend(k, 1)
        for t in range(EXT // 128):
            lxt[pl.ds(t * 128, 128), pl.ds(k * 2 * TOK, 2 * TOK)] = (
                lx_s[pl.ds(k * 2 * TOK, 2 * TOK), pl.ds(t * 128, 128)].astype(F32).T.astype(BF16)
            )

    def forward(n, j):
        got(1 + 2 * j, agb.at[1, j, c])
        send(5 + 2 * j, agb.at[1, j, c, pl.ds(0, CUT)], agb.at[3, j, c, pl.ds(0, CUT)], to_xp)
        send(n, agb.at[1, j, c], agb.at[1, j, c], to_sib)
        got(2 + 2 * j, agb.at[2, j, c])
        send(6 + 2 * j, agb.at[2, j, c, pl.ds(CUT, BLK - CUT)],
             agb.at[3, j, c, pl.ds(CUT, BLK - CUT)], to_xm)
        send(n + 1, agb.at[2, j, c], agb.at[2, j, c], to_sib)

    got(0, agb.at[0, 1, c])
    send(3, agb.at[0, 1, c], agb.at[1, 1, c], to_xp)
    send(4, agb.at[0, 1, c], agb.at[2, 1, c], to_xm)
    send(9, agb.at[0, 1, c], agb.at[0, 1, c], to_sib)
    forward(10, 0)
    got(9, agb.at[0, 1, sib])
    attend_pair(0)
    forward(12, 1)
    got(10, agb.at[1, 0, sib])
    got(12, agb.at[1, 1, sib])
    attend_pair(1)
    for j in range(2):
        got(5 + 2 * j, agb.at[3, j, c, pl.ds(0, CUT)])
        got(6 + 2 * j, agb.at[3, j, c, pl.ds(CUT, BLK - CUT)])
        send(14 + j, agb.at[3, j, c], agb.at[3, j, c], to_sib)
    got(11, agb.at[2, 0, sib])
    got(13, agb.at[2, 1, sib])
    attend_pair(2)
    got(14, agb.at[3, 0, sib])
    got(15, agb.at[3, 1, sib])
    attend_pair(3)

    top = mb[0]
    for b in range(1, 8):
        top = jnp.maximum(top, mb[b])
    total = jnp.zeros_like(top)
    for b in range(8):
        share = jnp.exp(mb[b] - top)
        mb[b] = share
        total = total + lb[b] * share
    inv = 1.0 / total
    for b in range(8):
        w = st[b] * (mb[b] * inv)[:1]
        st[b] = w
        wt[pl.ds(b * TOK, TOK), :] = w.astype(BF16)

    dots = jnp.zeros((1, ROWS), F32)
    for t in range(4):
        part = dot(lxt[pl.ds(t * 128, 128), :], wt[...])
        dots = dots + jnp.sum(
            gxt[pl.ds(t * 128, 128), :].astype(F32) * part, axis=0, keepdims=True
        )
        lot[pl.ds(t * 128, 128), :] = part.astype(BF16)

    def ring_first(n, buf, halves, dst):
        lo, hi = halves
        send(n, buf.at[x2].at[lo], dst[0], to_xp)
        send(n + 1, buf.at[x2].at[hi], dst[1], to_xm)
        send(n + 2, buf.at[xp].at[hi], dst[2], to_xp)
        send(n + 3, buf.at[xm].at[lo], dst[4], to_xm)

    def ring_second(n, buf, halves, dst, keep):
        lo, hi = halves
        got(n, dst[0])
        keep[0] = (buf[xp, lo].astype(F32) + dst[0][...].astype(F32)).astype(BF16)
        send(n + 4, keep.at[0], dst[3], to_xp)
        got(n + 1, dst[1])
        keep[1] = (buf[xm, hi].astype(F32) + dst[1][...].astype(F32)).astype(BF16)
        send(n + 5, keep.at[1], dst[5], to_xm)

    def ring_last(n, own_lo, own_hi, dst):
        got(n + 2, dst[2])
        got(n + 3, dst[4])
        got(n + 4, dst[3])
        got(n + 5, dst[5])
        low = own_lo.astype(F32) + dst[3][...].astype(F32) + dst[4][...].astype(F32)
        high = own_hi.astype(F32) + dst[2][...].astype(F32) + dst[5][...].astype(F32)
        return low, high

    v_part = dot(gotx[...], lot[...], 1, 1).astype(BF16)
    for a in range(8):
        for h in range(2):
            vb[a // 4, a % 4, pl.ds(16 * h, 16), :] = v_part[DN * h + 16 * a:DN * h + 16 * a + 16]
    send(41, vb.at[1 - yl], vry, to_y)

    for b in range(8):
        gst[pl.ds(b * TOK, TOK), :] = (st[b] * (gw[b] - dots) * scale).astype(BF16)
    rope_rows = None
    for t in range(5):
        part = dot(lxt[pl.ds(t * 128, 128), :], gst[...])
        if t < 4:
            gat[pl.ds(t * 128, 128), :] = part.astype(BF16)
        else:
            rope_rows = (part[:DR] + part[DR:]).astype(BF16)
    gr_ref[0] = rope_rows[:, :TOK]
    gr_ref[1] = rope_rows[:, TOK:]

    k_part = dot(qtx[...], gat[...], 1, 1).astype(BF16)
    for a in range(8):
        for h in range(2):
            kb[a // 2, a % 2, pl.ds(16 * h, 16), :] = k_part[DN * h + 16 * a:DN * h + 16 * a + 16]
    k_dst = (kr2p, kr2m, kra1, kra2, krb1, krb2)
    k_half = (0, 1)
    ring_first(53, kb, k_half, k_dst)

    def terms(k, j):
        start = pl.multiple_of((2 * k + j) * TOK, TOK)
        g = gst[pl.ds(start, TOK), :]
        full = dot(g, ax[...])
        lat = full[:, :DL] + dot(wt[pl.ds(start, TOK), :], gx[...])
        rope = jnp.where(low_lane, full[:HALF, DL:], full[HALF:, DL:])
        return lat, rope

    def put_terms(lat, rope, dst):
        for i in range(NZ):
            dst[pl.ds(96 * i, 96), :] = jnp.concatenate(
                [lat[24 * i:24 * i + 24, 128 * t:128 * t + 128] for t in range(4)], axis=0
            ).astype(dst.dtype)
        dst[pl.ds(96 * NZ, 96), :] = rope.astype(dst.dtype)

    def both_cores(k, dst):
        got(16 + k, crecv.at[k])
        dst[...] = (cown[k] + crecv[k].astype(F32)).astype(dst.dtype)

    x_dst = (r2p, r2m, ra1, ra2, rb1, rb2)
    low_rows, high_rows = pl.ds(0, CHH), pl.ds(CHH, CHH)

    for n, k in enumerate((3, 2, 1, 0)):
        put_terms(*terms(k, sib), csend.at[k])
        send(16 + k, csend.at[k], crecv.at[k], to_sib)
        put_terms(*terms(k, c), cown.at[k])
        if n == 1:
            both_cores(3, xs.at[3])
            send(20, xs.at[3, low_rows], r2p, to_xp)
            send(21, xs.at[3, high_rows], r2m, to_xm)
        if n == 2:
            both_cores(2, xs.at[2])
            send(22, xs.at[2, high_rows], ra1, to_xp)
        if n == 3:
            both_cores(1, xs.at[1])
            send(23, xs.at[1, low_rows], rb1, to_xm)
    got(20, r2p)
    xs[0, low_rows] = (xs[2, low_rows].astype(F32) + r2p[...].astype(F32)).astype(BF16)
    send(24, xs.at[0, low_rows], ra2, to_xp)
    got(21, r2m)
    xs[0, high_rows] = (xs[1, high_rows].astype(F32) + r2m[...].astype(F32)).astype(BF16)
    send(25, xs.at[0, high_rows], rb2, to_xm)
    both_cores(0, xsum)

    got(41, vry)
    vs[...] = (vb[yl].astype(F32) + vry[...].astype(F32)).astype(BF16)
    v_dst = (vr2p, vr2m, vra1, vra2, vrb1, vrb2)
    v_half = (pl.ds(0, 16), pl.ds(16, 16))
    ring_first(42, vs, v_half, v_dst)
    ring_second(53, kb, k_half, k_dst, kkeep)

    grad_nope = dot(gat[...], kup2, 0, 1)
    gn_ref[0] = grad_nope[:TOK, :DN].astype(BF16)
    gn_ref[1] = grad_nope[TOK:, DN:].astype(BF16)

    ring_second(42, vs, v_half, v_dst, vkeep)

    got(22, ra1)
    got(23, rb1)
    got(24, ra2)
    got(25, rb2)
    xsum[low_rows] = xsum[low_rows] + ra2[...].astype(F32) + rb1[...].astype(F32)
    xsum[high_rows] = xsum[high_rows] + ra1[...].astype(F32) + rb2[...].astype(F32)
    pad = jnp.zeros((8, 128), F32)
    for i in range(NZ):
        zs[i] = jnp.concatenate(
            [xsum[pl.ds(96 * i, 96)], xsum[pl.ds(96 * NZ + 24 * (i % 4), 24)], pad], axis=0
        ).astype(BF16)
    for d in range(1, NZ):
        far = (z + d) % NZ
        send(25 + d, zs.at[far], zrecv.at[d], device(z_=far))

    low, high = ring_last(53, kb[x, 0], kb[x, 1], k_dst)
    kx[0] = low.astype(BF16)
    kx[1] = high.astype(BF16)
    send(59, kx.at[1 - yl], kry, to_y)
    low, high = ring_last(42, vs[x, pl.ds(0, 16)], vs[x, pl.ds(16, 16)], v_dst)
    vfin[yl, x, pl.ds(0, 16)] = low.astype(BF16)
    vfin[yl, x, pl.ds(16, 16)] = high.astype(BF16)
    send(48, vfin.at[yl, x], vfin.at[yl, x], to_xp)
    send(49, vfin.at[yl, x], vfin.at[yl, x], to_xm)
    got(59, kry)
    kfin[x, yl] = (kx[yl].astype(F32) + kry[...].astype(F32)).astype(BF16)
    send(60, kfin.at[x, yl], kfin.at[x, yl], to_y)
    got(48, vfin.at[yl, xm])
    send(50, vfin.at[yl, xm, pl.ds(0, 16)], vfin.at[yl, xm, pl.ds(0, 16)], to_xp)
    got(49, vfin.at[yl, xp])
    send(51, vfin.at[yl, xp, pl.ds(16, 16)], vfin.at[yl, xp, pl.ds(16, 16)], to_xm)
    got(60, kfin.at[x, 1 - yl])
    send(61, kfin.at[x], kfin.at[x], to_xp)
    send(62, kfin.at[x], kfin.at[x], to_xm)
    got(50, vfin.at[yl, x2, pl.ds(0, 16)])
    got(51, vfin.at[yl, x2, pl.ds(16, 16)])
    send(52, vfin.at[yl], vfin.at[yl], to_y)

    zsum = zs[z].astype(F32)
    for d in range(1, NZ):
        got(25 + d, zrecv.at[d])
        zsum = zsum + zrecv[d].astype(F32)
    out_row, in_row = iota((128, 128), 0), iota((128, 128), 1)
    owner, place = out_row // 16, out_row % 16
    source = 24 * third(place) + 3 * owner + (place - 3 * third(place))
    order = jnp.where((source == in_row) & (place < 15), 1.0, 0.0).astype(BF16)
    sorted_rows = dot(order, zsum.astype(BF16)).astype(BF16)
    for i in range(8):
        ys[i] = sorted_rows[16 * i:16 * i + 16]

    def to_owner(d, e):
        far = (yh + d) % NYH
        return pltpu.make_async_remote_copy(
            src_ref=ys.at[far * 2 + e], dst_ref=yrecv.at[d, c],
            send_sem=ss.at[33 + 2 * d + e], recv_sem=rs.at[33 + 2 * d + c],
            device_id=device(yh_=far, yl_=(yl + c) % 2, c_=e), device_id_type=MESH,
        )

    for d in range(NYH):
        for e in range(2):
            if d == 0 and e == 0:
                @pl.when(c == 0)
                def _():
                    yrecv[0, 0] = ys[yh * 2]

                @pl.when(c == 1)
                def _():
                    to_owner(0, 0).start()
            else:
                to_owner(d, e).start()

    got(61, kfin.at[xm])
    send(63, kfin.at[xm, 0], kfin.at[xm, 0], to_xp)
    got(62, kfin.at[xp])
    send(64, kfin.at[xp, 1], kfin.at[xp, 1], to_xm)

    total = jnp.zeros((16, 128), F32)
    for d in range(NYH):
        for e in range(2):
            if d == 0 and e == 0:
                @pl.when(c == 1)
                def _():
                    got(33, yrecv.at[0, 0])
            else:
                got(33 + 2 * d + e, yrecv.at[d, e])
    for d in range(NYH):
        for e in range(2):
            total = total + yrecv[d, e].astype(F32)
    ol_ref[...] = jnp.concatenate([total[3 * t:3 * t + 3] for t in range(4)], axis=1).astype(BF16)
    rope = total[12:15]
    or_ref[...] = jnp.where(z >= NZ // 2, rope[:, DR:], rope[:, :DR]).astype(BF16)

    got(52, vfin.at[1 - yl])
    for a in range(8):
        for h in range(2):
            gv_ref[h, pl.ds(16 * a, 16), :] = vfin[a // 4, a % 4, pl.ds(16 * h, 16), :].astype(F32)
    got(63, kfin.at[x2, 0])
    got(64, kfin.at[x2, 1])
    for a in range(8):
        for h in range(2):
            gk_ref[h, pl.ds(16 * a, 16), :] = kfin[a // 2, a % 2, pl.ds(16 * h, 16), :].astype(F32)

    for copy in sent:
        copy.wait_send()
    for d in range(NYH):
        for e in range(2):
            if d == 0 and e == 0:
                @pl.when(c == 1)
                def _():
                    to_owner(0, 0).wait_send()
            else:
                to_owner(d, e).wait_send()


def on_device(query_nope, query_rope, grad_output, latents, key_rope, key_up, value_up, pair_order):
    scratch = [
        ((2, TOK, DN), BF16), ((2, DR, TOK), BF16), ((2, TOK, DN), BF16), ((DR, TOK), BF16),
        ((2, DN, DL), BF16), ((2, DN, DL), BF16), ((1, PAIRS), jnp.int32),
        ((4, 2, 2, BLK, 128), BF16), ((NX * 2 * TOK, EXT), BF16), ((EXT, NX * 2 * TOK), BF16),
        ((ROWS, EXT), BF16), ((EXT, ROWS), BF16), ((ROWS, DL), BF16), ((DL, ROWS), BF16),
        ((2 * DN, ROWS), BF16), ((2 * DN, ROWS), BF16),
        ((8, TOK, 128), F32), ((8, ROWS), F32), ((8, TOK, ROWS), F32), ((8, TOK, ROWS), F32),
        ((8, 8, ROWS), F32), ((8, 8, ROWS), F32),
        ((8 * TOK, ROWS), BF16), ((8 * TOK, ROWS), BF16), ((DL, ROWS), BF16), ((DL, ROWS), BF16),
        ((4, CH, 128), BF16), ((4, CH, 128), BF16), ((4, CH, 128), F32), ((4, CH, 128), BF16),
        ((CH, 128), F32),
        ((CHH, 128), BF16), ((CHH, 128), BF16), ((CHH, 128), BF16), ((CHH, 128), BF16),
        ((CHH, 128), BF16), ((CHH, 128), BF16),
        ((8, 128, 128), BF16), ((8, 128, 128), BF16), ((8, 16, 128), BF16), ((4, 2, 16, 128), BF16),
        ((2, 4, 32, DL), BF16), ((4, 32, DL), BF16), ((4, 32, DL), BF16),
    ] + [((16, DL), BF16)] * 6 + [((2, 4, 32, DL), BF16), ((2, 16, DL), BF16), ((4, 2, 32, DL), BF16)] + [
        ((32, DL), BF16)] * 6 + [
        ((2, 32, DL), BF16), ((2, 32, DL), BF16), ((32, DL), BF16), ((4, 2, 32, DL), BF16),
    ]
    outs = (
        ((2, TOK, DN), BF16), ((2, DR, TOK), BF16), ((3, DL), BF16), ((3, DR), BF16),
        ((2, DN, DL), F32), ((2, DN, DL), F32),
    )
    any_spec = pl.BlockSpec(memory_space=pl.ANY)
    vmem_spec = pl.BlockSpec(memory_space=pltpu.VMEM)
    grad_nope, grad_rope, own_lat, own_rope, grad_kup, grad_vup = pl.pallas_call(
        kernel,
        out_shape=[jax.ShapeDtypeStruct(s, t) for s, t in outs],
        in_specs=[any_spec] * 8,
        out_specs=[vmem_spec] * 6,
        scratch_shapes=[pltpu.VMEM(s, t) for s, t in scratch] + [
            pltpu.SemaphoreType.DMA((15,)),
            pltpu.SemaphoreType.DMA((N_SEM,)),
            pltpu.SemaphoreType.DMA((N_SEM,)),
        ],
        compiler_params=pltpu.CompilerParams(
            collective_id=0, has_side_effects=True, vmem_limit_bytes=60 * 1024 * 1024
        ),
        name="mla_backward",
    )(
        jnp.transpose(query_nope, (1, 0, 2)),
        jnp.transpose(query_rope, (1, 2, 0)),
        jnp.transpose(grad_output, (1, 0, 2)),
        latents,
        key_rope.T,
        key_up,
        value_up,
        pair_order.reshape(1, -1),
    )
    return (
        jnp.transpose(grad_nope, (1, 0, 2)),
        jnp.transpose(grad_rope, (2, 0, 1)),
        own_lat,
        own_rope,
        grad_kup,
        grad_vup,
    )


def solution(mesh):
    placed = (
        P("dp", "ctx", None),
        P("dp", "ctx", None),
        P("dp", "ctx", None),
        P("dp", None),
        P("dp", None),
        P("ctx", None, None),
        P("ctx", None, None),
        P(),
    )
    return jax.shard_map(
        on_device,
        mesh=mesh,
        in_specs=placed,
        out_specs=(
            P("dp", "ctx", None),
            P("dp", "ctx", None),
            P(("dp", "ctx"), None),
            P(("dp", "ctx"), None),
            P("ctx", None, None),
            P("ctx", None, None),
        ),
        check_vma=False,
    )
```

time: 292 us -> 70.1 us (0.24); the launches traced: 288 us -> 69.8 us
  blocking collectives: 139 us -> 0 us
  waiting for transfers between devices: 95.6 us -> 0 us
  Pallas kernels: 0 us -> 61.3 us
  matrix products: 25.9 us -> 0 us
  between operations: 14.3 us -> 0.65 us
    unnamed x1 -> x0, blocking collectives: 115 us -> none
    psum x1 -> x0, waiting for transfers between devices: 70.3 us -> none  [on_device(): lax.psum(grad_kup.astype(jnp.bfloat16), 'dp').astype(jnp.float32)]
    pallas_call x0 -> x1, Pallas kernels: none -> 61.3 us  [on_device(): pl.pallas_call(kernel, out_shape=[jax.ShapeDtypeStruct(s, t) for s, t in...]
    dot_general x14 -> x0, matrix products: 25.9 us -> none  [the longest x1 3.52 us: attend_local(): jnp.einsum('qhu,ul->qhl', weights_bf, all_latents, preferred_element_type...]
    all_gather x1 -> x0, waiting for transfers between devices: 24.6 us -> none  [on_device(): lax.all_gather(latents, 'dp', axis=0, tiled=True)]
    all_gather x1 -> x0, blocking collectives: 23.8 us -> none  [on_device(): lax.all_gather(key_rope, 'dp', axis=0, tiled=True)]
    unnamed x32 -> x14, local copies, waits for them, and re-layouts: 5.9 us -> 6.27 us
  transfers between devices with their start and end apart: 2 -> 0, of which waited for: 2 -> 0; matrix products, arithmetic and copies ran while one was open for 5% -> 0% of each run, Pallas kernels for 0% -> 0%
where the time goes in v1:
time: 70.1 us; the launch traced here: 69.8 us
  Pallas kernels  61.3 us (87%)
  local copies, waits for them, and re-layouts  7.91 us (11%)
    pallas_call x1, Pallas kernels, on_device(): pl.pallas_call(kernel, out_shape=[jax.ShapeDtypeStruct(s, t) for s, t in...  61.3 us
    unnamed x14, local copies, waits for them, and re-layouts  6.27 us
    transpose x1, local copies, waits for them, and re-layouts, on_device(): jnp.transpose(grad_output, (1, 0, 2))  1.64 us

profile of v1, /device:TPU:1, one launch (start us, length us, event | category | flops | bytes accessed | tf_op | source)
XLA Modules:
  0.0 69.8 jit_solution(17872199476699176702)
XLA Ops:
  0.6 1.6 %copy_bitcast_fusion = (bf16[2,192,128]{2,1,0:T(8,128)(2,1)}, bf16[2,192,128]{2,1,0:T(8,128)(2,1)}) fusion(bf16[192,2,128]{2,1,0:T(2,128)(2,1)} %param.10, bf16[192,2,128]{2,1,0:T(2,128)(2,1)} %param.8), kind=kLoop, calls=%fused_computation | loop fusion | bytes 393216 | tf_op jit(solution)/shard_map/transpose | solution.py:544
  2.3 61.3 %mla_backward.1 = (bf16[2,192,128]{2,1,0:T(8,128)(2,1)}, bf16[2,64,192]{2,1,0:T(8,128)(2,1)}, bf16[3,512]{1,0:T(4,128)(2,1)}, bf16[3,64]{1,0:T(4,128)(2,1)}, f32...) custom-call(bf16[2,192,128]{2,1,0:T(8,128)(2,1)} %get-tuple-element.25.q_hbm, bf16[2,64,192]{2,1,0:T(8,128)(2,1)} %bitcast.10, ...), custom_call_target="tpu_custom_call" | custom-call | tf_op jit(solution)/shard_map/mla_backward/pallas_call | solution.py:527
  63.6 0.0 copy-start.1
  63.6 1.7 %copy.16 = bf16[192,2,128]{2,1,0:T(2,128)(2,1)} copy(bf16[192,2,128]{2,0,1:T(8,128)(2,1)} %bitcast.9) | data formatting | bytes 196608
  65.2 0.0 copy-done.1
  65.2 0.0 copy-start.2
  65.2 0.6 copy.24
  65.9 0.0 copy-done.2
  65.9 0.0 copy-start.3
  65.9 0.6 copy.25
  66.5 0.0 copy-done.3
  66.6 0.6 copy.26
  67.1 0.0 copy-start
  67.1 1.9 %copy.27 = f32[2,128,512]{2,1,0:T(8,128)} copy(f32[2,128,512]{2,1,0:T(8,128)} %get-tuple-element.36) | data formatting | bytes 1048576
  69.0 0.0 copy-done
  69.0 0.8 %copy.28 = f32[2,128,512]{2,1,0:T(8,128)} copy(f32[2,128,512]{2,1,0:T(8,128)S(1)} %copy-done) | data formatting | bytes 1048576
Async XLA Ops:
  63.6 1.7 %copy-start.1 = (bf16[2,64,192]{2,1,0:T(8,128)(2,1)S(1)}, bf16[2,64,192]{2,1,0:T(8,128)(2,1)}, u32[]{:S(2)}) copy-start(bf16[2,64,192]{2,1,0:T(8,128)(2,1)} %get-tuple-element.13) | copy-start | bytes 147460
  65.2 0.7 copy-start.2
  65.9 0.6 copy-start.3
  67.1 1.9 %copy-start = (f32[2,128,512]{2,1,0:T(8,128)S(1)}, f32[2,128,512]{2,1,0:T(8,128)}, u32[]{:S(2)}) copy-start(f32[2,128,512]{2,1,0:T(8,128)} %get-tuple-element.37) | copy-start | bytes 1572868

commit v2 on v1

--- a/solution.py
+++ b/solution.py
@@ -45,14 +45,14 @@
 
 def kernel(
     q_hbm, qr_hbm, go_hbm, lat_hbm, kr_hbm, kup_hbm, vup_hbm, po_hbm,
-    gn_ref, gr_ref, ol_ref, or_ref, gk_ref, gv_ref,
+    gn_ref, gr_ref, ol_ref, or_ref, kfin, vfin,
     q_v, qr_v, go_v, kr_v, kup_v, vup_v, po_v,
     agb, lx_s, lxt, ax, axt, gx, gxt, qtx, gotx,
     pcol, prow, st, gw, mb, lb, wt, gst, lot, gat,
     csend, crecv, cown, xs, xsum, r2p, r2m, ra1, ra2, rb1, rb2,
     zs, zrecv, ys, yrecv,
-    vb, vry, vs, vr2p, vr2m, vra1, vra2, vrb1, vrb2, vfin,
-    vkeep, kb, kr2p, kr2m, kra1, kra2, krb1, krb2, kkeep, kx, kry, kfin,
+    vb, vry, vs, vr2p, vr2m, vra1, vra2, vrb1, vrb2,
+    vkeep, kb, kr2p, kr2m, kra1, kra2, krb1, krb2, kkeep, kx, kry,
     lsem, ss, rs,
 ):
     dp, ctx = lax.axis_index("dp"), lax.axis_index("ctx")
@@ -146,8 +146,9 @@
     blank = jnp.zeros((TOK, DN), F32)
 
     def block_diagonal(ref):
-        top = jnp.concatenate([ref[0].astype(F32), blank], axis=1)
-        low = jnp.concatenate([blank, ref[1].astype(F32)], axis=1)
+        both = ref[...].astype(F32)
+        top = jnp.concatenate([both[:, 0, :], blank], axis=1)
+        low = jnp.concatenate([blank, both[:, 1, :]], axis=1)
         return jnp.concatenate([top, low], axis=0)
 
     qx = block_diagonal(q_v)
@@ -477,15 +478,8 @@
     or_ref[...] = jnp.where(z >= NZ // 2, rope[:, DR:], rope[:, :DR]).astype(BF16)
 
     got(52, vfin.at[1 - yl])
-    for a in range(8):
-        for h in range(2):
-            gv_ref[h, pl.ds(16 * a, 16), :] = vfin[a // 4, a % 4, pl.ds(16 * h, 16), :].astype(F32)
     got(63, kfin.at[x2, 0])
     got(64, kfin.at[x2, 1])
-    for a in range(8):
-        for h in range(2):
-            gk_ref[h, pl.ds(16 * a, 16), :] = kfin[a // 2, a % 2, pl.ds(16 * h, 16), :].astype(F32)
-
     for copy in sent:
         copy.wait_send()
     for d in range(NYH):
@@ -498,9 +492,20 @@
                 to_owner(d, e).wait_send()
 
 
+def finish(gn_in, gr_in, ol_in, or_in, kfin, vfin, gn_ref, gr_ref, ol_ref, or_ref, gk_ref, gv_ref):
+    gr_ref[...] = gr_in[...]
+    ol_ref[...] = ol_in[...]
+    or_ref[...] = or_in[...]
+    for a in range(8):
+        for h in range(2):
+            gk_ref[h, pl.ds(16 * a, 16), :] = kfin[a // 2, a % 2, pl.ds(16 * h, 16), :].astype(F32)
+            gv_ref[h, pl.ds(16 * a, 16), :] = vfin[a // 4, a % 4, pl.ds(16 * h, 16), :].astype(F32)
+    gn_ref[...] = jnp.stack([gn_in[0].astype(F32), gn_in[1].astype(F32)], axis=1).astype(BF16)
+
+
 def on_device(query_nope, query_rope, grad_output, latents, key_rope, key_up, value_up, pair_order):
     scratch = [
-        ((2, TOK, DN), BF16), ((2, DR, TOK), BF16), ((2, TOK, DN), BF16), ((DR, TOK), BF16),
+        ((TOK, 2, DN), BF16), ((2, DR, TOK), BF16), ((TOK, 2, DN), BF16), ((DR, TOK), BF16),
         ((2, DN, DL), BF16), ((2, DN, DL), BF16), ((1, PAIRS), jnp.int32),
         ((4, 2, 2, BLK, 128), BF16), ((NX * 2 * TOK, EXT), BF16), ((EXT, NX * 2 * TOK), BF16),
         ((ROWS, EXT), BF16), ((EXT, ROWS), BF16), ((ROWS, DL), BF16), ((DL, ROWS), BF16),
@@ -514,17 +519,17 @@
         ((CHH, 128), BF16), ((CHH, 128), BF16),
         ((8, 128, 128), BF16), ((8, 128, 128), BF16), ((8, 16, 128), BF16), ((4, 2, 16, 128), BF16),
         ((2, 4, 32, DL), BF16), ((4, 32, DL), BF16), ((4, 32, DL), BF16),
-    ] + [((16, DL), BF16)] * 6 + [((2, 4, 32, DL), BF16), ((2, 16, DL), BF16), ((4, 2, 32, DL), BF16)] + [
+    ] + [((16, DL), BF16)] * 6 + [((2, 16, DL), BF16), ((4, 2, 32, DL), BF16)] + [
         ((32, DL), BF16)] * 6 + [
-        ((2, 32, DL), BF16), ((2, 32, DL), BF16), ((32, DL), BF16), ((4, 2, 32, DL), BF16),
+        ((2, 32, DL), BF16), ((2, 32, DL), BF16), ((32, DL), BF16),
     ]
     outs = (
         ((2, TOK, DN), BF16), ((2, DR, TOK), BF16), ((3, DL), BF16), ((3, DR), BF16),
-        ((2, DN, DL), F32), ((2, DN, DL), F32),
+        ((4, 2, 32, DL), BF16), ((2, 4, 32, DL), BF16),
     )
     any_spec = pl.BlockSpec(memory_space=pl.ANY)
     vmem_spec = pl.BlockSpec(memory_space=pltpu.VMEM)
-    grad_nope, grad_rope, own_lat, own_rope, grad_kup, grad_vup = pl.pallas_call(
+    raw = pl.pallas_call(
         kernel,
         out_shape=[jax.ShapeDtypeStruct(s, t) for s, t in outs],
         in_specs=[any_spec] * 8,
@@ -539,23 +544,27 @@
         ),
         name="mla_backward",
     )(
-        jnp.transpose(query_nope, (1, 0, 2)),
+        query_nope,
         jnp.transpose(query_rope, (1, 2, 0)),
-        jnp.transpose(grad_output, (1, 0, 2)),
+        grad_output,
         latents,
         key_rope.T,
         key_up,
         value_up,
         pair_order.reshape(1, -1),
     )
-    return (
-        jnp.transpose(grad_nope, (1, 0, 2)),
-        jnp.transpose(grad_rope, (2, 0, 1)),
-        own_lat,
-        own_rope,
-        grad_kup,
-        grad_vup,
+    results = (
+        ((TOK, 2, DN), BF16), ((2, DR, TOK), BF16), ((3, DL), BF16), ((3, DR), BF16),
+        ((2, DN, DL), F32), ((2, DN, DL), F32),
     )
+    grad_nope, grad_rope, own_lat, own_rope, grad_kup, grad_vup = pl.pallas_call(
+        finish,
+        out_shape=[jax.ShapeDtypeStruct(s, t) for s, t in results],
+        in_specs=[vmem_spec] * 6,
+        out_specs=[vmem_spec] * 6,
+        name="finish",
+    )(*raw)
+    return grad_nope, jnp.transpose(grad_rope, (2, 0, 1)), own_lat, own_rope, grad_kup, grad_vup
 
 
 def solution(mesh):

time: 70.1 us -> 64 us (0.913)
  local copies, waits for them, and re-layouts: 7.91 us -> 0 us
  Pallas kernels: 61.3 us -> 63.2 us
    unnamed x14 -> x0, local copies, waits for them, and re-layouts: 6.27 us -> none
    pallas_call x0 -> x1, Pallas kernels: none -> 2.19 us  [on_device(): pl.pallas_call(finish, out_shape=[jax.ShapeDtypeStruct(s, t) for s, t in...]
    transpose x1 -> x0, local copies, waits for them, and re-layouts: 1.64 us -> none  [on_device(): jnp.transpose(grad_output, (1, 0, 2))]
where the time goes in v2:
time: 64 us; the launch traced here: 63.8 us
  Pallas kernels  63.2 us (99%)
  between operations  0.64 us (1%)
    pallas_call x1, Pallas kernels, on_device(): pl.pallas_call(kernel, out_shape=[jax.ShapeDtypeStruct(s, t) for s, t in...  61 us
    pallas_call x1, Pallas kernels, on_device(): pl.pallas_call(finish, out_shape=[jax.ShapeDtypeStruct(s, t) for s, t in...  2.19 us

profile of v2, /device:TPU:1, one launch (start us, length us, event | category | flops | bytes accessed | tf_op | source)
XLA Modules:
  0.0 63.8 jit_solution(5807815826760004160)
XLA Ops:
  0.6 61.0 %mla_backward.1 = (bf16[2,192,128]{2,1,0:T(8,128)(2,1)}, bf16[2,64,192]{2,1,0:T(8,128)(2,1)}, bf16[3,512]{1,0:T(4,128)(2,1)}, bf16[3,64]{1,0:T(4,128)(2,1)}, bf1...) custom-call(bf16[192,2,128]{2,1,0:T(2,128)(2,1)} %q_hbm.1, bf16[2,64,192]{2,1,0:T(8,128)(2,1)} %bitcast.4, ...), custom_call_target="tpu_custom_call" | custom-call | tf_op jit(solution)/shard_map/mla_backward/pallas_call | solution.py:532
  61.6 2.2 %finish.1 = (bf16[192,2,128]{2,1,0:T(2,128)(2,1)}, bf16[2,64,192]{2,1,0:T(8,128)(2,1)}, bf16[3,512]{1,0:T(4,128)(2,1)}, bf16[3,64]{1,0:T(4,128)(2,1)}, f32[2,128,512]{2,1,0:T(8,128)}, /*index=5*/f32[2,128,512]{2,1,0:T(8,128)}) custom-call(bf16[2,192,128]{2,1,0:T(8,128)(2,1)} %get-tuple-element.18.gn_in, bf16[2,64,192]{2,1,0:T(8,128)(2,1)} %get-tuple-element.19.gr_in, ...), custom_call_target="tpu_custom_call" | custom-call | tf_op jit(solution)/shard_map/finish/pallas_call | solution.py:560

commit v3 on v2

--- a/solution.py
+++ b/solution.py
@@ -28,7 +28,7 @@
 
 REL = (0, 3, 1, 2)
 
-N_SEM = 65
+N_SEM = 69
 
 
 def dot(a, b, ca=1, cb=0):
@@ -51,9 +51,9 @@
     pcol, prow, st, gw, mb, lb, wt, gst, lot, gat,
     csend, crecv, cown, xs, xsum, r2p, r2m, ra1, ra2, rb1, rb2,
     zs, zrecv, ys, yrecv,
-    vb, vry, vs, vr2p, vr2m, vra1, vra2, vrb1, vrb2,
-    vkeep, kb, kr2p, kr2m, kra1, kra2, krb1, krb2, kkeep, kx, kry,
-    lsem, ss, rs,
+    vb, vry, vs, vr2p, vr2m, vra1, vra2, vrb1, vrb2, vkeep,
+    kb, kry, ks, kr2p, kr2m, kra1, kra2, krb1, krb2, kkeep,
+    lsem, ss, rs, known,
 ):
     dp, ctx = lax.axis_index("dp"), lax.axis_index("ctx")
     x, yl = dp // NYL, dp % NYL
@@ -88,20 +88,21 @@
 
     barrier = pltpu.get_barrier_semaphore()
 
-    def greet(dev):
+    row = yh * 2 + yl
+    along_y = []
+    for step in (1, 7):
+        far = (row + step) % (2 * NYH)
+        along_y.append(device(yl_=far % 2, yh_=far // 2))
+    along_z = [device(z_=(z + step) % NZ) for step in (1, NZ - 1)]
+    for dev in [to_sib, to_xp, to_xm] + along_y + along_z:
         pl.semaphore_signal(barrier, inc=1, device_id=dev, device_id_type=MESH)
 
-    greet(to_xp)
-    greet(to_xm)
-    greet(device(yl_=1 - yl))
-    for d in range(NYH):
-        far = (yh + d) % NYH
-        greet(device(yh_=far, c_=sib))
-        greet(device(yh_=far, yl_=1 - yl, c_=sib))
-        if d:
-            greet(device(yh_=far, yl_=(yl + c) % 2, c_=c))
-    for d in range(1, NZ):
-        greet(device(z_=(z + d) % NZ))
+    def tell(n):
+        for dev in along_y + along_z:
+            pl.semaphore_signal(known.at[n], inc=1, device_id=dev, device_id_type=MESH)
+
+    def heard(n):
+        pl.semaphore_wait(known.at[n], 4)
 
     local = []
 
@@ -131,11 +132,12 @@
     for copy in lat_in:
         copy.wait()
 
-    pl.semaphore_wait(barrier, 21)
+    pl.semaphore_wait(barrier, 7)
 
     send(0, agb.at[0, 0, c], agb.at[0, 1, c], to_y)
     send(1, agb.at[0, 0, c], agb.at[1, 0, c], to_xp)
     send(2, agb.at[0, 0, c], agb.at[2, 0, c], to_xm)
+    tell(0)
 
     q_in.wait()
     go_in.wait()
@@ -233,14 +235,20 @@
              agb.at[3, j, c, pl.ds(CUT, BLK - CUT)], to_xm)
         send(n + 1, agb.at[2, j, c], agb.at[2, j, c], to_sib)
 
+    heard(0)
+    tell(1)
     got(0, agb.at[0, 1, c])
     send(3, agb.at[0, 1, c], agb.at[1, 1, c], to_xp)
     send(4, agb.at[0, 1, c], agb.at[2, 1, c], to_xm)
     send(9, agb.at[0, 1, c], agb.at[0, 1, c], to_sib)
     forward(10, 0)
+    heard(1)
+    tell(2)
     got(9, agb.at[0, 1, sib])
     attend_pair(0)
     forward(12, 1)
+    heard(2)
+    tell(3)
     got(10, agb.at[1, 0, sib])
     got(12, agb.at[1, 1, sib])
     attend_pair(1)
@@ -254,6 +262,7 @@
     got(14, agb.at[3, 0, sib])
     got(15, agb.at[3, 1, sib])
     attend_pair(3)
+    heard(3)
 
     top = mb[0]
     for b in range(1, 8):
@@ -293,40 +302,44 @@
         keep[1] = (buf[xm, hi].astype(F32) + dst[1][...].astype(F32)).astype(BF16)
         send(n + 5, keep.at[1], dst[5], to_xm)
 
-    def ring_last(n, own_lo, own_hi, dst):
+    def ring_last(n, buf, halves, dst, fin):
         got(n + 2, dst[2])
         got(n + 3, dst[4])
         got(n + 4, dst[3])
         got(n + 5, dst[5])
-        low = own_lo.astype(F32) + dst[3][...].astype(F32) + dst[4][...].astype(F32)
-        high = own_hi.astype(F32) + dst[2][...].astype(F32) + dst[5][...].astype(F32)
-        return low, high
-
-    v_part = dot(gotx[...], lot[...], 1, 1).astype(BF16)
-    for a in range(8):
-        for h in range(2):
-            vb[a // 4, a % 4, pl.ds(16 * h, 16), :] = v_part[DN * h + 16 * a:DN * h + 16 * a + 16]
-    send(41, vb.at[1 - yl], vry, to_y)
+        for half, one, two in zip(halves, dst[3:1:-1], dst[4:6]):
+            fin[yl, x, half] = (
+                buf[x, half].astype(F32) + one[...].astype(F32) + two[...].astype(F32)
+            ).astype(BF16)
+
+    halves = (pl.ds(0, 16), pl.ds(16, 16))
+    v_dst = (vr2p, vr2m, vra1, vra2, vrb1, vrb2)
+    k_dst = (kr2p, kr2m, kra1, kra2, krb1, krb2)
+
+    def to_pair(n, part, buf, dst):
+        for a in range(8):
+            for h in range(2):
+                buf[a // 4, a % 4, pl.ds(16 * h, 16), :] = part[DN * h + 16 * a:DN * h + 16 * a + 16]
+        send(n, buf.at[1 - yl], dst, to_y)
+
+    def from_pair(n, buf, other, total):
+        got(n, other)
+        total[...] = (buf[yl].astype(F32) + other[...].astype(F32)).astype(BF16)
+
+    def peers():
+        for n, (dx, dy) in enumerate(((1, 0), (3, 0), (0, 1), (2, 0), (1, 1), (3, 1), (2, 1))):
+            yield n, (x + dx) % NX, (x + NX - dx) % NX, (yl + dy) % 2
+
+    def spread(n, fin):
+        for i, to_x, _, side in peers():
+            send(n + i, fin.at[yl, x], fin.at[yl, x], device(x_=to_x, yl_=side))
+
+    def spread_got(n, fin):
+        for i, _, from_x, side in peers():
+            got(n + i, fin.at[side, from_x])
 
     for b in range(8):
         gst[pl.ds(b * TOK, TOK), :] = (st[b] * (gw[b] - dots) * scale).astype(BF16)
-    rope_rows = None
-    for t in range(5):
-        part = dot(lxt[pl.ds(t * 128, 128), :], gst[...])
-        if t < 4:
-            gat[pl.ds(t * 128, 128), :] = part.astype(BF16)
-        else:
-            rope_rows = (part[:DR] + part[DR:]).astype(BF16)
-    gr_ref[0] = rope_rows[:, :TOK]
-    gr_ref[1] = rope_rows[:, TOK:]
-
-    k_part = dot(qtx[...], gat[...], 1, 1).astype(BF16)
-    for a in range(8):
-        for h in range(2):
-            kb[a // 2, a % 2, pl.ds(16 * h, 16), :] = k_part[DN * h + 16 * a:DN * h + 16 * a + 16]
-    k_dst = (kr2p, kr2m, kra1, kra2, krb1, krb2)
-    k_half = (0, 1)
-    ring_first(53, kb, k_half, k_dst)
 
     def terms(k, j):
         start = pl.multiple_of((2 * k + j) * TOK, TOK)
@@ -347,23 +360,29 @@
         got(16 + k, crecv.at[k])
         dst[...] = (cown[k] + crecv[k].astype(F32)).astype(dst.dtype)
 
-    x_dst = (r2p, r2m, ra1, ra2, rb1, rb2)
     low_rows, high_rows = pl.ds(0, CHH), pl.ds(CHH, CHH)
 
-    for n, k in enumerate((3, 2, 1, 0)):
+    def chunk(k):
         put_terms(*terms(k, sib), csend.at[k])
         send(16 + k, csend.at[k], crecv.at[k], to_sib)
         put_terms(*terms(k, c), cown.at[k])
-        if n == 1:
-            both_cores(3, xs.at[3])
-            send(20, xs.at[3, low_rows], r2p, to_xp)
-            send(21, xs.at[3, high_rows], r2m, to_xm)
-        if n == 2:
-            both_cores(2, xs.at[2])
-            send(22, xs.at[2, high_rows], ra1, to_xp)
-        if n == 3:
-            both_cores(1, xs.at[1])
-            send(23, xs.at[1, low_rows], rb1, to_xm)
+
+    chunk(3)
+    to_pair(41, dot(gotx[...], lot[...], 1, 1).astype(BF16), vb, vry)
+    chunk(2)
+    both_cores(3, xs.at[3])
+    send(20, xs.at[3, low_rows], r2p, to_xp)
+    send(21, xs.at[3, high_rows], r2m, to_xm)
+    chunk(1)
+    both_cores(2, xs.at[2])
+    send(22, xs.at[2, high_rows], ra1, to_xp)
+    chunk(0)
+    both_cores(1, xs.at[1])
+    send(23, xs.at[1, low_rows], rb1, to_xm)
+
+    gat[...] = dot(lxt[:DL, :], gst[...]).astype(BF16)
+    to_pair(48, dot(qtx[...], gat[...], 1, 1).astype(BF16), kb, kry)
+
     got(20, r2p)
     xs[0, low_rows] = (xs[2, low_rows].astype(F32) + r2p[...].astype(F32)).astype(BF16)
     send(24, xs.at[0, low_rows], ra2, to_xp)
@@ -372,18 +391,20 @@
     send(25, xs.at[0, high_rows], rb2, to_xm)
     both_cores(0, xsum)
 
-    got(41, vry)
-    vs[...] = (vb[yl].astype(F32) + vry[...].astype(F32)).astype(BF16)
-    v_dst = (vr2p, vr2m, vra1, vra2, vrb1, vrb2)
-    v_half = (pl.ds(0, 16), pl.ds(16, 16))
-    ring_first(42, vs, v_half, v_dst)
-    ring_second(53, kb, k_half, k_dst, kkeep)
-
+    from_pair(41, vb, vry, vs)
+    ring_first(42, vs, halves, v_dst)
+
+    rope2 = dot(lxt[DL:, :], gst[...])
+    rope_rows = (rope2[:DR] + rope2[DR:]).astype(BF16)
+    gr_ref[0] = rope_rows[:, :TOK]
+    gr_ref[1] = rope_rows[:, TOK:]
     grad_nope = dot(gat[...], kup2, 0, 1)
     gn_ref[0] = grad_nope[:TOK, :DN].astype(BF16)
     gn_ref[1] = grad_nope[TOK:, DN:].astype(BF16)
 
-    ring_second(42, vs, v_half, v_dst, vkeep)
+    from_pair(48, kb, kry, ks)
+    ring_first(49, ks, halves, k_dst)
+    ring_second(42, vs, halves, v_dst, vkeep)
 
     got(22, ra1)
     got(23, rb1)
@@ -396,41 +417,24 @@
         zs[i] = jnp.concatenate(
             [xsum[pl.ds(96 * i, 96)], xsum[pl.ds(96 * NZ + 24 * (i % 4), 24)], pad], axis=0
         ).astype(BF16)
-    for d in range(1, NZ):
+    for d in (4, 3, 5, 2, 6, 1, 7):
         far = (z + d) % NZ
         send(25 + d, zs.at[far], zrecv.at[d], device(z_=far))
 
-    low, high = ring_last(53, kb[x, 0], kb[x, 1], k_dst)
-    kx[0] = low.astype(BF16)
-    kx[1] = high.astype(BF16)
-    send(59, kx.at[1 - yl], kry, to_y)
-    low, high = ring_last(42, vs[x, pl.ds(0, 16)], vs[x, pl.ds(16, 16)], v_dst)
-    vfin[yl, x, pl.ds(0, 16)] = low.astype(BF16)
-    vfin[yl, x, pl.ds(16, 16)] = high.astype(BF16)
-    send(48, vfin.at[yl, x], vfin.at[yl, x], to_xp)
-    send(49, vfin.at[yl, x], vfin.at[yl, x], to_xm)
-    got(59, kry)
-    kfin[x, yl] = (kx[yl].astype(F32) + kry[...].astype(F32)).astype(BF16)
-    send(60, kfin.at[x, yl], kfin.at[x, yl], to_y)
-    got(48, vfin.at[yl, xm])
-    send(50, vfin.at[yl, xm, pl.ds(0, 16)], vfin.at[yl, xm, pl.ds(0, 16)], to_xp)
-    got(49, vfin.at[yl, xp])
-    send(51, vfin.at[yl, xp, pl.ds(16, 16)], vfin.at[yl, xp, pl.ds(16, 16)], to_xm)
-    got(60, kfin.at[x, 1 - yl])
-    send(61, kfin.at[x], kfin.at[x], to_xp)
-    send(62, kfin.at[x], kfin.at[x], to_xm)
-    got(50, vfin.at[yl, x2, pl.ds(0, 16)])
-    got(51, vfin.at[yl, x2, pl.ds(16, 16)])
-    send(52, vfin.at[yl], vfin.at[yl], to_y)
-
-    zsum = zs[z].astype(F32)
-    for d in range(1, NZ):
-        got(25 + d, zrecv.at[d])
-        zsum = zsum + zrecv[d].astype(F32)
+    ring_last(42, vs, halves, v_dst, vfin)
+    spread(55, vfin)
+    ring_second(49, ks, halves, k_dst, kkeep)
+    ring_last(49, ks, halves, k_dst, kfin)
+    spread(62, kfin)
+
     out_row, in_row = iota((128, 128), 0), iota((128, 128), 1)
     owner, place = out_row // 16, out_row % 16
     source = 24 * third(place) + 3 * owner + (place - 3 * third(place))
     order = jnp.where((source == in_row) & (place < 15), 1.0, 0.0).astype(BF16)
+    zsum = zs[z].astype(F32)
+    for d in (1, 7, 2, 6, 3, 5, 4):
+        got(25 + d, zrecv.at[d])
+        zsum = zsum + zrecv[d].astype(F32)
     sorted_rows = dot(order, zsum.astype(BF16)).astype(BF16)
     for i in range(8):
         ys[i] = sorted_rows[16 * i:16 * i + 16]
@@ -456,10 +460,8 @@
             else:
                 to_owner(d, e).start()
 
-    got(61, kfin.at[xm])
-    send(63, kfin.at[xm, 0], kfin.at[xm, 0], to_xp)
-    got(62, kfin.at[xp])
-    send(64, kfin.at[xp, 1], kfin.at[xp, 1], to_xm)
+    spread_got(55, vfin)
+    spread_got(62, kfin)
 
     total = jnp.zeros((16, 128), F32)
     for d in range(NYH):
@@ -477,9 +479,6 @@
     rope = total[12:15]
     or_ref[...] = jnp.where(z >= NZ // 2, rope[:, DR:], rope[:, :DR]).astype(BF16)
 
-    got(52, vfin.at[1 - yl])
-    got(63, kfin.at[x2, 0])
-    got(64, kfin.at[x2, 1])
     for copy in sent:
         copy.wait_send()
     for d in range(NYH):
@@ -498,7 +497,7 @@
     or_ref[...] = or_in[...]
     for a in range(8):
         for h in range(2):
-            gk_ref[h, pl.ds(16 * a, 16), :] = kfin[a // 2, a % 2, pl.ds(16 * h, 16), :].astype(F32)
+            gk_ref[h, pl.ds(16 * a, 16), :] = kfin[a // 4, a % 4, pl.ds(16 * h, 16), :].astype(F32)
             gv_ref[h, pl.ds(16 * a, 16), :] = vfin[a // 4, a % 4, pl.ds(16 * h, 16), :].astype(F32)
     gn_ref[...] = jnp.stack([gn_in[0].astype(F32), gn_in[1].astype(F32)], axis=1).astype(BF16)
 
@@ -518,14 +517,12 @@
         ((CHH, 128), BF16), ((CHH, 128), BF16), ((CHH, 128), BF16), ((CHH, 128), BF16),
         ((CHH, 128), BF16), ((CHH, 128), BF16),
         ((8, 128, 128), BF16), ((8, 128, 128), BF16), ((8, 16, 128), BF16), ((4, 2, 16, 128), BF16),
-        ((2, 4, 32, DL), BF16), ((4, 32, DL), BF16), ((4, 32, DL), BF16),
-    ] + [((16, DL), BF16)] * 6 + [((2, 16, DL), BF16), ((4, 2, 32, DL), BF16)] + [
-        ((32, DL), BF16)] * 6 + [
-        ((2, 32, DL), BF16), ((2, 32, DL), BF16), ((32, DL), BF16),
-    ]
+    ] + (
+        [((2, 4, 32, DL), BF16)] + [((4, 32, DL), BF16)] * 2 + [((16, DL), BF16)] * 6 + [((2, 16, DL), BF16)]
+    ) * 2
     outs = (
         ((2, TOK, DN), BF16), ((2, DR, TOK), BF16), ((3, DL), BF16), ((3, DR), BF16),
-        ((4, 2, 32, DL), BF16), ((2, 4, 32, DL), BF16),
+        ((2, 4, 32, DL), BF16), ((2, 4, 32, DL), BF16),
     )
     any_spec = pl.BlockSpec(memory_space=pl.ANY)
     vmem_spec = pl.BlockSpec(memory_space=pltpu.VMEM)
@@ -538,6 +535,7 @@
             pltpu.SemaphoreType.DMA((15,)),
             pltpu.SemaphoreType.DMA((N_SEM,)),
             pltpu.SemaphoreType.DMA((N_SEM,)),
+            pltpu.SemaphoreType.REGULAR((4,)),
         ],
         compiler_params=pltpu.CompilerParams(
             collective_id=0, has_side_effects=True, vmem_limit_bytes=60 * 1024 * 1024

time: 64 us -> 62 us (0.969)
  Pallas kernels: 63.2 us -> 61.2 us
    pallas_call x1, Pallas kernels: 61 us -> 59 us  [on_device(): pl.pallas_call(kernel, out_shape=[jax.ShapeDtypeStruct(s, t) for s, t in...]
where the time goes in v3:
time: 62 us; the launch traced here: 61.9 us
  Pallas kernels  61.2 us (99%)
  between operations  0.64 us (1%)
    pallas_call x1, Pallas kernels, on_device(): pl.pallas_call(kernel, out_shape=[jax.ShapeDtypeStruct(s, t) for s, t in...  59 us
    pallas_call x1, Pallas kernels, on_device(): pl.pallas_call(finish, out_shape=[jax.ShapeDtypeStruct(s, t) for s, t in...  2.19 us

profile of v3, /device:TPU:1, one launch (start us, length us, event | category | flops | bytes accessed | tf_op | source)
XLA Modules:
  0.0 61.9 jit_solution(7485844324069711264)
XLA Ops:
  0.6 59.0 %mla_backward.1 = (bf16[2,192,128]{2,1,0:T(8,128)(2,1)}, bf16[2,64,192]{2,1,0:T(8,128)(2,1)}, bf16[3,512]{1,0:T(4,128)(2,1)}, bf16[3,64]{1,0:T(4,128)(2,1)}, bf1...) custom-call(bf16[192,2,128]{2,1,0:T(2,128)(2,1)} %q_hbm.1, bf16[2,64,192]{2,1,0:T(8,128)(2,1)} %bitcast.4, ...), custom_call_target="tpu_custom_call" | custom-call | tf_op jit(solution)/shard_map/mla_backward/pallas_call | solution.py:529
  59.7 2.2 %finish.1 = (bf16[192,2,128]{2,1,0:T(2,128)(2,1)}, bf16[2,64,192]{2,1,0:T(8,128)(2,1)}, bf16[3,512]{1,0:T(4,128)(2,1)}, bf16[3,64]{1,0:T(4,128)(2,1)}, f32[2,128,512]{2,1,0:T(8,128)}, /*index=5*/f32[2,128,512]{2,1,0:T(8,128)}) custom-call(bf16[2,192,128]{2,1,0:T(8,128)(2,1)} %get-tuple-element.18.gn_in, bf16[2,64,192]{2,1,0:T(8,128)(2,1)} %get-tuple-element.19.gr_in, ...), custom_call_target="tpu_custom_call" | custom-call | tf_op jit(solution)/shard_map/finish/pallas_call | solution.py:558

commit v4 on v3

--- a/solution.py
+++ b/solution.py
@@ -28,7 +28,7 @@
 
 REL = (0, 3, 1, 2)
 
-N_SEM = 69
+N_SEM = 101
 
 
 def dot(a, b, ca=1, cb=0):
@@ -134,9 +134,40 @@
 
     pl.semaphore_wait(barrier, 7)
 
-    send(0, agb.at[0, 0, c], agb.at[0, 1, c], to_y)
-    send(1, agb.at[0, 0, c], agb.at[1, 0, c], to_xp)
-    send(2, agb.at[0, 0, c], agb.at[2, 0, c], to_xm)
+    far = (row + 1 + 6 * c) % (2 * NYH)
+    to_yg = device(yl_=far % 2, yh_=far // 2)
+    pieces = (pl.ds(0, CUT), pl.ds(CUT, BLK - CUT))
+    x_id, y_id, sib_id = 0, 16, 32
+
+    def block(k, j, p, core=c):
+        return agb.at[k, j, core, pieces[p]]
+
+    def gather_x(k, j, p, source):
+        dst = block(k, j, p)
+        send(x_id + 4 * k + 2 * j + p, source, dst, to_xp if (k, p) in ((1, 0), (1, 1), (3, 0)) else to_xm)
+
+    def gather_y(k, p):
+        send(y_id + 2 * k + p, block(k, 0, p), block(k, 1, p), to_yg)
+
+    def gather_sib(k, j, p):
+        send(sib_id + 4 * k + 2 * j + p, block(k, j, p), block(k, j, p), to_sib)
+
+    def from_x(k, j, p):
+        got(x_id + 4 * k + 2 * j + p, block(k, j, p))
+
+    def from_y(k, p):
+        got(y_id + 2 * k + p, block(k, 1, p))
+
+    def from_sib(k, j):
+        for p in range(2):
+            got(sib_id + 4 * k + 2 * j + p, block(k, j, p, sib))
+
+    gather_x(1, 0, 0, block(0, 0, 0))
+    gather_x(2, 0, 1, block(0, 0, 1))
+    gather_y(0, 0)
+    gather_x(1, 0, 1, block(0, 0, 1))
+    gather_x(2, 0, 0, block(0, 0, 0))
+    gather_y(0, 1)
     tell(0)
 
     q_in.wait()
@@ -165,10 +196,10 @@
     qr2 = jnp.concatenate([qr_rows, qr_rows], axis=1)
     ax[:, :DL] = absorbed.astype(BF16)
     ax[:, DL:] = qr2.astype(BF16)
-    axt[:DL, :] = absorbed.T.astype(BF16)
-    axt[DL:, :] = qr2.T.astype(BF16)
+    axt[:DL, :] = absorbed.astype(BF16).T
+    axt[DL:, :] = qr2.astype(BF16).T
     gx[...] = grad_lat.astype(BF16)
-    gxt[...] = grad_lat.T.astype(BF16)
+    gxt[...] = grad_lat.astype(BF16).T
 
     po_row = jnp.broadcast_to(po_v[...].astype(F32), (8, PAIRS))
     slot_t = third(iota((PAIRS, ROWS), 1) % HALF)
@@ -218,50 +249,67 @@
         mb[b] = jnp.broadcast_to(m, (8, ROWS))
         lb[b] = jnp.broadcast_to(jnp.sum(p, axis=0, keepdims=True), (8, ROWS))
 
-    def attend_pair(k):
-        attend(k, 0)
-        attend(k, 1)
+    def turn(k):
         for t in range(EXT // 128):
             lxt[pl.ds(t * 128, 128), pl.ds(k * 2 * TOK, 2 * TOK)] = (
-                lx_s[pl.ds(k * 2 * TOK, 2 * TOK), pl.ds(t * 128, 128)].astype(F32).T.astype(BF16)
+                lx_s[pl.ds(k * 2 * TOK, 2 * TOK), pl.ds(t * 128, 128)].T
             )
 
-    def forward(n, j):
-        got(1 + 2 * j, agb.at[1, j, c])
-        send(5 + 2 * j, agb.at[1, j, c, pl.ds(0, CUT)], agb.at[3, j, c, pl.ds(0, CUT)], to_xp)
-        send(n, agb.at[1, j, c], agb.at[1, j, c], to_sib)
-        got(2 + 2 * j, agb.at[2, j, c])
-        send(6 + 2 * j, agb.at[2, j, c, pl.ds(CUT, BLK - CUT)],
-             agb.at[3, j, c, pl.ds(CUT, BLK - CUT)], to_xm)
-        send(n + 1, agb.at[2, j, c], agb.at[2, j, c], to_sib)
+    def on_from_x(k, p):
+        from_x(k, 0, p)
+        if (k, p) in ((1, 0), (2, 1)):
+            gather_x(3, 0, p, block(k, 0, p))
+        gather_y(k, p)
+        gather_sib(k, 0, p)
+
+    def on_from_y(k, p):
+        from_y(k, p)
+        if (k, p) in ((1, 0), (2, 1)):
+            gather_x(3, 1, p, block(k, 1, p))
+        gather_sib(k, 1, p)
+
+    def on_far(j):
+        for p in range(2):
+            from_x(3, j, p)
+            gather_sib(3, j, p)
 
     heard(0)
     tell(1)
-    got(0, agb.at[0, 1, c])
-    send(3, agb.at[0, 1, c], agb.at[1, 1, c], to_xp)
-    send(4, agb.at[0, 1, c], agb.at[2, 1, c], to_xm)
-    send(9, agb.at[0, 1, c], agb.at[0, 1, c], to_sib)
-    forward(10, 0)
+    on_from_x(1, 0)
+    on_from_x(2, 1)
+    on_from_y(0, 0)
+    on_from_y(0, 1)
     heard(1)
     tell(2)
-    got(9, agb.at[0, 1, sib])
-    attend_pair(0)
-    forward(12, 1)
+    attend(0, 0)
+    on_from_x(1, 1)
+    on_from_x(2, 0)
     heard(2)
     tell(3)
-    got(10, agb.at[1, 0, sib])
-    got(12, agb.at[1, 1, sib])
-    attend_pair(1)
-    for j in range(2):
-        got(5 + 2 * j, agb.at[3, j, c, pl.ds(0, CUT)])
-        got(6 + 2 * j, agb.at[3, j, c, pl.ds(CUT, BLK - CUT)])
-        send(14 + j, agb.at[3, j, c], agb.at[3, j, c], to_sib)
-    got(11, agb.at[2, 0, sib])
-    got(13, agb.at[2, 1, sib])
-    attend_pair(2)
-    got(14, agb.at[3, 0, sib])
-    got(15, agb.at[3, 1, sib])
-    attend_pair(3)
+    from_sib(0, 1)
+    attend(0, 1)
+    on_from_y(1, 0)
+    on_from_y(2, 1)
+    turn(0)
+    on_far(0)
+    from_sib(1, 0)
+    attend(1, 0)
+    on_from_y(1, 1)
+    on_from_y(2, 0)
+    from_sib(2, 0)
+    attend(2, 0)
+    from_sib(3, 0)
+    attend(3, 0)
+    on_far(1)
+    from_sib(1, 1)
+    attend(1, 1)
+    turn(1)
+    from_sib(2, 1)
+    attend(2, 1)
+    turn(2)
+    from_sib(3, 1)
+    attend(3, 1)
+    turn(3)
     heard(3)
 
     top = mb[0]
@@ -357,42 +405,42 @@
         dst[pl.ds(96 * NZ, 96), :] = rope.astype(dst.dtype)
 
     def both_cores(k, dst):
-        got(16 + k, crecv.at[k])
+        got(48 + k, crecv.at[k])
         dst[...] = (cown[k] + crecv[k].astype(F32)).astype(dst.dtype)
 
     low_rows, high_rows = pl.ds(0, CHH), pl.ds(CHH, CHH)
 
     def chunk(k):
         put_terms(*terms(k, sib), csend.at[k])
-        send(16 + k, csend.at[k], crecv.at[k], to_sib)
+        send(48 + k, csend.at[k], crecv.at[k], to_sib)
         put_terms(*terms(k, c), cown.at[k])
 
     chunk(3)
-    to_pair(41, dot(gotx[...], lot[...], 1, 1).astype(BF16), vb, vry)
+    to_pair(73, dot(gotx[...], lot[...], 1, 1).astype(BF16), vb, vry)
     chunk(2)
     both_cores(3, xs.at[3])
-    send(20, xs.at[3, low_rows], r2p, to_xp)
-    send(21, xs.at[3, high_rows], r2m, to_xm)
+    send(52, xs.at[3, low_rows], r2p, to_xp)
+    send(53, xs.at[3, high_rows], r2m, to_xm)
     chunk(1)
     both_cores(2, xs.at[2])
-    send(22, xs.at[2, high_rows], ra1, to_xp)
+    send(54, xs.at[2, high_rows], ra1, to_xp)
     chunk(0)
     both_cores(1, xs.at[1])
-    send(23, xs.at[1, low_rows], rb1, to_xm)
+    send(55, xs.at[1, low_rows], rb1, to_xm)
 
     gat[...] = dot(lxt[:DL, :], gst[...]).astype(BF16)
-    to_pair(48, dot(qtx[...], gat[...], 1, 1).astype(BF16), kb, kry)
-
-    got(20, r2p)
+    to_pair(80, dot(qtx[...], gat[...], 1, 1).astype(BF16), kb, kry)
+
+    got(52, r2p)
     xs[0, low_rows] = (xs[2, low_rows].astype(F32) + r2p[...].astype(F32)).astype(BF16)
-    send(24, xs.at[0, low_rows], ra2, to_xp)
-    got(21, r2m)
+    send(56, xs.at[0, low_rows], ra2, to_xp)
+    got(53, r2m)
     xs[0, high_rows] = (xs[1, high_rows].astype(F32) + r2m[...].astype(F32)).astype(BF16)
-    send(25, xs.at[0, high_rows], rb2, to_xm)
+    send(57, xs.at[0, high_rows], rb2, to_xm)
     both_cores(0, xsum)
 
-    from_pair(41, vb, vry, vs)
-    ring_first(42, vs, halves, v_dst)
+    from_pair(73, vb, vry, vs)
+    ring_first(74, vs, halves, v_dst)
 
     rope2 = dot(lxt[DL:, :], gst[...])
     rope_rows = (rope2[:DR] + rope2[DR:]).astype(BF16)
@@ -402,14 +450,13 @@
     gn_ref[0] = grad_nope[:TOK, :DN].astype(BF16)
     gn_ref[1] = grad_nope[TOK:, DN:].astype(BF16)
 
-    from_pair(48, kb, kry, ks)
-    ring_first(49, ks, halves, k_dst)
-    ring_second(42, vs, halves, v_dst, vkeep)
-
-    got(22, ra1)
-    got(23, rb1)
-    got(24, ra2)
-    got(25, rb2)
+    from_pair(80, kb, kry, ks)
+    ring_first(81, ks, halves, k_dst)
+
+    got(54, ra1)
+    got(55, rb1)
+    got(56, ra2)
+    got(57, rb2)
     xsum[low_rows] = xsum[low_rows] + ra2[...].astype(F32) + rb1[...].astype(F32)
     xsum[high_rows] = xsum[high_rows] + ra1[...].astype(F32) + rb2[...].astype(F32)
     pad = jnp.zeros((8, 128), F32)
@@ -419,13 +466,14 @@
         ).astype(BF16)
     for d in (4, 3, 5, 2, 6, 1, 7):
         far = (z + d) % NZ
-        send(25 + d, zs.at[far], zrecv.at[d], device(z_=far))
-
-    ring_last(42, vs, halves, v_dst, vfin)
-    spread(55, vfin)
-    ring_second(49, ks, halves, k_dst, kkeep)
-    ring_last(49, ks, halves, k_dst, kfin)
-    spread(62, kfin)
+        send(57 + d, zs.at[far], zrecv.at[d], device(z_=far))
+
+    ring_second(74, vs, halves, v_dst, vkeep)
+    ring_second(81, ks, halves, k_dst, kkeep)
+    ring_last(74, vs, halves, v_dst, vfin)
+    spread(87, vfin)
+    ring_last(81, ks, halves, k_dst, kfin)
+    spread(94, kfin)
 
     out_row, in_row = iota((128, 128), 0), iota((128, 128), 1)
     owner, place = out_row // 16, out_row % 16
@@ -433,7 +481,7 @@
     order = jnp.where((source == in_row) & (place < 15), 1.0, 0.0).astype(BF16)
     zsum = zs[z].astype(F32)
     for d in (1, 7, 2, 6, 3, 5, 4):
-        got(25 + d, zrecv.at[d])
+        got(57 + d, zrecv.at[d])
         zsum = zsum + zrecv[d].astype(F32)
     sorted_rows = dot(order, zsum.astype(BF16)).astype(BF16)
     for i in range(8):
@@ -443,7 +491,7 @@
         far = (yh + d) % NYH
         return pltpu.make_async_remote_copy(
             src_ref=ys.at[far * 2 + e], dst_ref=yrecv.at[d, c],
-            send_sem=ss.at[33 + 2 * d + e], recv_sem=rs.at[33 + 2 * d + c],
+            send_sem=ss.at[65 + 2 * d + e], recv_sem=rs.at[65 + 2 * d + c],
             device_id=device(yh_=far, yl_=(yl + c) % 2, c_=e), device_id_type=MESH,
         )
 
@@ -460,8 +508,8 @@
             else:
                 to_owner(d, e).start()
 
-    spread_got(55, vfin)
-    spread_got(62, kfin)
+    spread_got(87, vfin)
+    spread_got(94, kfin)
 
     total = jnp.zeros((16, 128), F32)
     for d in range(NYH):
@@ -469,9 +517,9 @@
             if d == 0 and e == 0:
                 @pl.when(c == 1)
                 def _():
-                    got(33, yrecv.at[0, 0])
+                    got(65, yrecv.at[0, 0])
             else:
-                got(33 + 2 * d + e, yrecv.at[d, e])
+                got(65 + 2 * d + e, yrecv.at[d, e])
     for d in range(NYH):
         for e in range(2):
             total = total + yrecv[d, e].astype(F32)

time: 62 us -> 60.3 us (0.973)
  Pallas kernels: 61.2 us -> 59.5 us
    pallas_call x1, Pallas kernels: 59 us -> 57.3 us  [on_device(): pl.pallas_call(kernel, out_shape=[jax.ShapeDtypeStruct(s, t) for s, t in...]
where the time goes in v4:
time: 60.3 us; the launch traced here: 60.1 us
  Pallas kernels  59.5 us (99%)
  between operations  0.64 us (1%)
    pallas_call x1, Pallas kernels, on_device(): pl.pallas_call(kernel, out_shape=[jax.ShapeDtypeStruct(s, t) for s, t in...  57.3 us
    pallas_call x1, Pallas kernels, on_device(): pl.pallas_call(finish, out_shape=[jax.ShapeDtypeStruct(s, t) for s, t in...  2.19 us

profile of v4, /device:TPU:1, one launch (start us, length us, event | category | flops | bytes accessed | tf_op | source)
XLA Modules:
  0.0 60.1 jit_solution(5982279605694636892)
XLA Ops:
  0.6 57.3 %mla_backward.1 = (bf16[2,192,128]{2,1,0:T(8,128)(2,1)}, bf16[2,64,192]{2,1,0:T(8,128)(2,1)}, bf16[3,512]{1,0:T(4,128)(2,1)}, bf16[3,64]{1,0:T(4,128)(2,1)}, bf1...) custom-call(bf16[192,2,128]{2,1,0:T(2,128)(2,1)} %q_hbm.1, bf16[2,64,192]{2,1,0:T(8,128)(2,1)} %bitcast.4, ...), custom_call_target="tpu_custom_call" | custom-call | tf_op jit(solution)/shard_map/mla_backward/pallas_call | solution.py:577
  58.0 2.2 %finish.1 = (bf16[192,2,128]{2,1,0:T(2,128)(2,1)}, bf16[2,64,192]{2,1,0:T(8,128)(2,1)}, bf16[3,512]{1,0:T(4,128)(2,1)}, bf16[3,64]{1,0:T(4,128)(2,1)}, f32[2,128,512]{2,1,0:T(8,128)}, /*index=5*/f32[2,128,512]{2,1,0:T(8,128)}) custom-call(bf16[2,192,128]{2,1,0:T(8,128)(2,1)} %get-tuple-element.18.gn_in, bf16[2,64,192]{2,1,0:T(8,128)(2,1)} %get-tuple-element.19.gr_in, ...), custom_call_target="tpu_custom_call" | custom-call | tf_op jit(solution)/shard_map/finish/pallas_call | solution.py:606

commit v5 on v4

--- a/solution.py
+++ b/solution.py
@@ -23,12 +23,13 @@
 PER_DEV = 32
 BLK = 4 * HALF + 48
 CUT = 224
-CH = NZ * 96 + 96
-CHH = CH // 2
+CHA = NZ * 72 + 96
+CHH = CHA // 2
+CH = CHA + TOK
 
 REL = (0, 3, 1, 2)
 
-N_SEM = 101
+N_SEM = 111
 
 
 def dot(a, b, ca=1, cb=0):
@@ -50,7 +51,7 @@
     agb, lx_s, lxt, ax, axt, gx, gxt, qtx, gotx,
     pcol, prow, st, gw, mb, lb, wt, gst, lot, gat,
     csend, crecv, cown, xs, xsum, r2p, r2m, ra1, ra2, rb1, rb2,
-    zs, zrecv, ys, yrecv,
+    zs, zrecv, bs, brecv, bx, bxr, ys, yrecv,
     vb, vry, vs, vr2p, vr2m, vra1, vra2, vrb1, vrb2, vkeep,
     kb, kry, ks, kr2p, kr2m, kra1, kra2, krb1, krb2, kkeep,
     lsem, ss, rs, known,
@@ -398,15 +399,17 @@
         return lat, rope
 
     def put_terms(lat, rope, dst):
-        for i in range(NZ):
-            dst[pl.ds(96 * i, 96), :] = jnp.concatenate(
-                [lat[24 * i:24 * i + 24, 128 * t:128 * t + 128] for t in range(4)], axis=0
+        for i in range(0, NZ, 2):
+            dst[pl.ds(72 * i, 144), :] = jnp.concatenate(
+                [lat[24 * r:24 * r + 24, 128 * t:128 * t + 128] for r in (i, i + 1) for t in range(3)], axis=0
             ).astype(dst.dtype)
-        dst[pl.ds(96 * NZ, 96), :] = rope.astype(dst.dtype)
+        dst[pl.ds(72 * NZ, 96), :] = rope.astype(dst.dtype)
+        dst[pl.ds(CHA, TOK), :] = lat[:, 384:].astype(dst.dtype)
 
     def both_cores(k, dst):
         got(48 + k, crecv.at[k])
-        dst[...] = (cown[k] + crecv[k].astype(F32)).astype(dst.dtype)
+        rows = pl.ds(0, CHA)
+        dst[...] = (cown[k, rows] + crecv[k, rows].astype(F32)).astype(dst.dtype)
 
     low_rows, high_rows = pl.ds(0, CHH), pl.ds(CHH, CHH)
 
@@ -438,6 +441,13 @@
     xs[0, high_rows] = (xs[1, high_rows].astype(F32) + r2m[...].astype(F32)).astype(BF16)
     send(57, xs.at[0, high_rows], rb2, to_xm)
     both_cores(0, xsum)
+    rows = pl.ds(CHA, TOK)
+    parts = [cown[k, rows] + crecv[k, rows].astype(F32) for k in range(NX)]
+    for i in range(NZ):
+        bs[i] = jnp.concatenate([part[24 * i:24 * i + 24] for part in parts], axis=0).astype(BF16)
+    for d in (4, 3, 5, 2, 6, 1, 7):
+        far = (z + d) % NZ
+        send(100 + d, bs.at[far], brecv.at[d], device(z_=far))
 
     from_pair(73, vb, vry, vs)
     ring_first(74, vs, halves, v_dst)
@@ -462,11 +472,19 @@
     pad = jnp.zeros((8, 128), F32)
     for i in range(NZ):
         zs[i] = jnp.concatenate(
-            [xsum[pl.ds(96 * i, 96)], xsum[pl.ds(96 * NZ + 24 * (i % 4), 24)], pad], axis=0
+            [xsum[pl.ds(72 * i, 72)], xsum[pl.ds(72 * NZ + 24 * (i % 4), 24)]], axis=0
         ).astype(BF16)
     for d in (4, 3, 5, 2, 6, 1, 7):
         far = (z + d) % NZ
         send(57 + d, zs.at[far], zrecv.at[d], device(z_=far))
+
+    fourth = bs[z].astype(F32)
+    for d in (1, 7, 2, 6, 3, 5, 4):
+        got(100 + d, brecv.at[d])
+        fourth = fourth + brecv[d].astype(F32)
+    for k, there, dev in ((3, 3, device(x_=x2)), (2, 1, to_xp), (1, 2, to_xm)):
+        bx[k] = jnp.concatenate([fourth[24 * k:24 * k + 24], pad], axis=0).astype(BF16)
+        send(107 + there, bx.at[k], bxr.at[there], dev)
 
     ring_second(74, vs, halves, v_dst, vkeep)
     ring_second(81, ks, halves, k_dst, kkeep)
@@ -479,10 +497,15 @@
     owner, place = out_row // 16, out_row % 16
     source = 24 * third(place) + 3 * owner + (place - 3 * third(place))
     order = jnp.where((source == in_row) & (place < 15), 1.0, 0.0).astype(BF16)
+    own = fourth[:24]
+    for k in range(1, NX):
+        got(107 + k, bxr.at[k])
+        own = own + bxr[k].astype(F32)[:24]
     zsum = zs[z].astype(F32)
     for d in (1, 7, 2, 6, 3, 5, 4):
         got(57 + d, zrecv.at[d])
         zsum = zsum + zrecv[d].astype(F32)
+    zsum = jnp.concatenate([zsum[:72], own, zsum[72:], pad], axis=0)
     sorted_rows = dot(order, zsum.astype(BF16)).astype(BF16)
     for i in range(8):
         ys[i] = sorted_rows[16 * i:16 * i + 16]
@@ -560,11 +583,12 @@
         ((8, TOK, 128), F32), ((8, ROWS), F32), ((8, TOK, ROWS), F32), ((8, TOK, ROWS), F32),
         ((8, 8, ROWS), F32), ((8, 8, ROWS), F32),
         ((8 * TOK, ROWS), BF16), ((8 * TOK, ROWS), BF16), ((DL, ROWS), BF16), ((DL, ROWS), BF16),
-        ((4, CH, 128), BF16), ((4, CH, 128), BF16), ((4, CH, 128), F32), ((4, CH, 128), BF16),
-        ((CH, 128), F32),
+        ((4, CH, 128), BF16), ((4, CH, 128), BF16), ((4, CH, 128), F32), ((4, CHA, 128), BF16),
+        ((CHA, 128), F32),
         ((CHH, 128), BF16), ((CHH, 128), BF16), ((CHH, 128), BF16), ((CHH, 128), BF16),
         ((CHH, 128), BF16), ((CHH, 128), BF16),
-        ((8, 128, 128), BF16), ((8, 128, 128), BF16), ((8, 16, 128), BF16), ((4, 2, 16, 128), BF16),
+        ((8, 96, 128), BF16), ((8, 96, 128), BF16), ((8, 96, 128), BF16), ((8, 96, 128), BF16),
+        ((4, 32, 128), BF16), ((4, 32, 128), BF16), ((8, 16, 128), BF16), ((4, 2, 16, 128), BF16),
     ] + (
         [((2, 4, 32, DL), BF16)] + [((4, 32, DL), BF16)] * 2 + [((16, DL), BF16)] * 6 + [((2, 16, DL), BF16)]
     ) * 2
@@ -576,7 +600,7 @@
     vmem_spec = pl.BlockSpec(memory_space=pltpu.VMEM)
     raw = pl.pallas_call(
         kernel,
-        out_shape=[jax.ShapeDtypeStruct(s, t) for s, t in outs],
+        out_shape=[pltpu.VMEM(s, t) for s, t in outs],
         in_specs=[any_spec] * 8,
         out_specs=[vmem_spec] * 6,
         scratch_shapes=[pltpu.VMEM(s, t) for s, t in scratch] + [
@@ -609,7 +633,7 @@
         in_specs=[vmem_spec] * 6,
         out_specs=[vmem_spec] * 6,
         name="finish",
-    )(*raw)
+    )(*[pltpu.with_memory_space_constraint(r, pltpu.VMEM) for r in raw])
     return grad_nope, jnp.transpose(grad_rope, (2, 0, 1)), own_lat, own_rope, grad_kup, grad_vup
 
 

time: 60.3 us -> 58.8 us (0.975)
  Pallas kernels: 59.5 us -> 58.1 us
    pallas_call x1, Pallas kernels: 2.19 us -> 1.08 us  [on_device(): pl.pallas_call(finish, out_shape=[jax.ShapeDtypeStruct(s, t) for s, t in...]
where the time goes in v5:
time: 58.8 us; the launch traced here: 58.7 us
  Pallas kernels  58.1 us (99%)
  between operations  0.64 us (1%)
    pallas_call x1, Pallas kernels, on_device(): pl.pallas_call(kernel, out_shape=[pltpu.VMEM(s, t) for s, t in outs], in_...  57 us

profile of v5, /device:TPU:1, one launch (start us, length us, event | category | flops | bytes accessed | tf_op | source)
XLA Modules:
  0.0 58.7 jit_solution(9434810407945443521)
XLA Ops:
  0.6 57.0 %mla_backward.1 = (bf16[2,192,128]{2,1,0:T(8,128)(2,1)S(1)}, bf16[2,64,192]{2,1,0:T(8,128)(2,1)S(1)}, bf16[3,512]{1,0:T(4,128)(2,1)S(1)}, bf16[3,64]{1,0:T(4,128...) custom-call(bf16[192,2,128]{2,1,0:T(2,128)(2,1)} %q_hbm.1, ...), custom_call_target="tpu_custom_call" | custom-call | tf_op jit(solution)/shard_map/mla_backward/pallas_call | solution.py:601
  57.6 1.1 %finish.1 = (bf16[192,2,128]{2,1,0:T(2,128)(2,1)}, bf16[2,64,192]{2,1,0:T(8,128)(2,1)}, bf16[3,512]{1,0:T(4,128)(2,1)}, bf16[3,64]{1,0:T(4,128)(2,1)}, f32[2,128,512]{2,1,0:T(8,128)}, /*index=5*/f32[2,128,512]{2,1,0:T(8,128)}) custom-call(bf16[2,192,128]{2,1,0:T(8,128)(2,1)S(1)} %get-tuple-element.18.gn_in, bf16[2,64,192]{2,1,0:T(8,128)(2,1)S(1)} %get-tuple-element.19.gr_in, ...), custom_call_target="tpu_custom_call" | custom-call | tf_op jit(solution)/shard_map/finish/pallas_call | solution.py:630

commit v6 on v5

--- a/solution.py
+++ b/solution.py
@@ -49,7 +49,7 @@
     gn_ref, gr_ref, ol_ref, or_ref, kfin, vfin,
     q_v, qr_v, go_v, kr_v, kup_v, vup_v, po_v,
     agb, lx_s, lxt, ax, axt, gx, gxt, qtx, gotx,
-    pcol, prow, st, gw, mb, lb, wt, gst, lot, gat,
+    pcol, prow, st, gw, mb, lb, lacc, mtop, wt, gst, lot, gat,
     csend, crecv, cown, xs, xsum, r2p, r2m, ra1, ra2, rb1, rb2,
     zs, zrecv, bs, brecv, bx, bxr, ys, yrecv,
     vb, vry, vs, vr2p, vr2m, vra1, vra2, vrb1, vrb2, vkeep,
@@ -125,45 +125,44 @@
     go_in, vup_in = fetch(go_hbm, go_v), fetch(vup_hbm, vup_v)
     qr_in, po_in = fetch(qr_hbm, qr_v), fetch(po_hbm, po_v)
 
+    for copy in lat_in:
+        copy.wait()
+    pl.semaphore_wait(barrier, 7)
+
+    far = (row + 1 + 6 * c) % (2 * NYH)
+    to_yg = device(yl_=far % 2, yh_=far // 2)
+    pieces = (pl.ds(0, CUT), pl.ds(CUT, BLK - CUT))
+    x_id, y_id, sib_id = 0, 16, 32
+
+    def block(k, j, p, core=c):
+        return agb.at[k, j, core, pieces[p]]
+
+    def gather_x(k, j, p, source):
+        dst = block(k, j, p)
+        send(x_id + 4 * k + 2 * j + p, source, dst, to_xp if (k, p) in ((1, 0), (1, 1), (3, 0)) else to_xm)
+
+    def gather_y(k, p):
+        send(y_id + 2 * k + p, block(k, 0, p), block(k, 1, p), to_yg)
+
+    def gather_sib(k, j, p):
+        send(sib_id + 4 * k + 2 * j + p, block(k, j, p), block(k, j, p), to_sib)
+
+    def from_x(k, j, p):
+        got(x_id + 4 * k + 2 * j + p, block(k, j, p))
+
+    def from_y(k, p):
+        got(y_id + 2 * k + p, block(k, 1, p))
+
+    def from_sib(k, j):
+        for p in range(2):
+            got(sib_id + 4 * k + 2 * j + p, block(k, j, p, sib))
+
+    gather_x(1, 0, 0, block(0, 0, 0))
     kr_in.wait()
     kr_own = kr_v[...].astype(F32).T
     krp = jnp.concatenate([kr_own[:HALF], kr_own[HALF:]], axis=1).astype(BF16)
     agb[0, 0, 0, pl.ds(4 * HALF, 48)] = krp[:48]
     agb[0, 0, 1, pl.ds(4 * HALF, 48)] = krp[48:]
-    for copy in lat_in:
-        copy.wait()
-
-    pl.semaphore_wait(barrier, 7)
-
-    far = (row + 1 + 6 * c) % (2 * NYH)
-    to_yg = device(yl_=far % 2, yh_=far // 2)
-    pieces = (pl.ds(0, CUT), pl.ds(CUT, BLK - CUT))
-    x_id, y_id, sib_id = 0, 16, 32
-
-    def block(k, j, p, core=c):
-        return agb.at[k, j, core, pieces[p]]
-
-    def gather_x(k, j, p, source):
-        dst = block(k, j, p)
-        send(x_id + 4 * k + 2 * j + p, source, dst, to_xp if (k, p) in ((1, 0), (1, 1), (3, 0)) else to_xm)
-
-    def gather_y(k, p):
-        send(y_id + 2 * k + p, block(k, 0, p), block(k, 1, p), to_yg)
-
-    def gather_sib(k, j, p):
-        send(sib_id + 4 * k + 2 * j + p, block(k, j, p), block(k, j, p), to_sib)
-
-    def from_x(k, j, p):
-        got(x_id + 4 * k + 2 * j + p, block(k, j, p))
-
-    def from_y(k, p):
-        got(y_id + 2 * k + p, block(k, 1, p))
-
-    def from_sib(k, j):
-        for p in range(2):
-            got(sib_id + 4 * k + 2 * j + p, block(k, j, p, sib))
-
-    gather_x(1, 0, 0, block(0, 0, 0))
     gather_x(2, 0, 1, block(0, 0, 1))
     gather_y(0, 0)
     gather_x(1, 0, 1, block(0, 0, 1))
@@ -255,6 +254,12 @@
             lxt[pl.ds(t * 128, 128), pl.ds(k * 2 * TOK, 2 * TOK)] = (
                 lx_s[pl.ds(k * 2 * TOK, 2 * TOK), pl.ds(t * 128, 128)].T
             )
+        top = jnp.maximum(mb[2 * k], mb[2 * k + 1])
+        both = [st[b] * jnp.exp(mb[b] - top)[:1] for b in (2 * k, 2 * k + 1)]
+        lacc[k] = dot(
+            lxt[pl.ds(0, DL), pl.ds(k * 2 * TOK, 2 * TOK)], jnp.concatenate(both, axis=0).astype(BF16)
+        )
+        mtop[k] = top
 
     def on_from_x(k, p):
         from_x(k, 0, p)
@@ -313,27 +318,22 @@
     turn(3)
     heard(3)
 
-    top = mb[0]
-    for b in range(1, 8):
-        top = jnp.maximum(top, mb[b])
+    top = jnp.maximum(jnp.maximum(mtop[0], mtop[1]), jnp.maximum(mtop[2], mtop[3]))
     total = jnp.zeros_like(top)
     for b in range(8):
         share = jnp.exp(mb[b] - top)
         mb[b] = share
         total = total + lb[b] * share
     inv = 1.0 / total
-    for b in range(8):
-        w = st[b] * (mb[b] * inv)[:1]
-        st[b] = w
-        wt[pl.ds(b * TOK, TOK), :] = w.astype(BF16)
-
+    parts = [(jnp.exp(mtop[k] - top) * inv)[:1] for k in range(NX)]
     dots = jnp.zeros((1, ROWS), F32)
     for t in range(4):
-        part = dot(lxt[pl.ds(t * 128, 128), :], wt[...])
-        dots = dots + jnp.sum(
-            gxt[pl.ds(t * 128, 128), :].astype(F32) * part, axis=0, keepdims=True
-        )
-        lot[pl.ds(t * 128, 128), :] = part.astype(BF16)
+        rows = pl.ds(t * 128, 128)
+        part = lacc[0, rows] * parts[0]
+        for k in range(1, NX):
+            part = part + lacc[k, rows] * parts[k]
+        dots = dots + jnp.sum(gxt[rows, :].astype(F32) * part, axis=0, keepdims=True)
+        lot[rows, :] = part.astype(BF16)
 
     def ring_first(n, buf, halves, dst):
         lo, hi = halves
@@ -388,7 +388,9 @@
             got(n + i, fin.at[side, from_x])
 
     for b in range(8):
-        gst[pl.ds(b * TOK, TOK), :] = (st[b] * (gw[b] - dots) * scale).astype(BF16)
+        w = st[b] * (mb[b] * inv)[:1]
+        wt[pl.ds(b * TOK, TOK), :] = w.astype(BF16)
+        gst[pl.ds(b * TOK, TOK), :] = (w * (gw[b] - dots) * scale).astype(BF16)
 
     def terms(k, j):
         start = pl.multiple_of((2 * k + j) * TOK, TOK)
@@ -478,6 +480,9 @@
         far = (z + d) % NZ
         send(57 + d, zs.at[far], zrecv.at[d], device(z_=far))
 
+    ring_second(74, vs, halves, v_dst, vkeep)
+    ring_second(81, ks, halves, k_dst, kkeep)
+
     fourth = bs[z].astype(F32)
     for d in (1, 7, 2, 6, 3, 5, 4):
         got(100 + d, brecv.at[d])
@@ -486,8 +491,6 @@
         bx[k] = jnp.concatenate([fourth[24 * k:24 * k + 24], pad], axis=0).astype(BF16)
         send(107 + there, bx.at[k], bxr.at[there], dev)
 
-    ring_second(74, vs, halves, v_dst, vkeep)
-    ring_second(81, ks, halves, k_dst, kkeep)
     ring_last(74, vs, halves, v_dst, vfin)
     spread(87, vfin)
     ring_last(81, ks, halves, k_dst, kfin)
@@ -581,7 +584,7 @@
         ((ROWS, EXT), BF16), ((EXT, ROWS), BF16), ((ROWS, DL), BF16), ((DL, ROWS), BF16),
         ((2 * DN, ROWS), BF16), ((2 * DN, ROWS), BF16),
         ((8, TOK, 128), F32), ((8, ROWS), F32), ((8, TOK, ROWS), F32), ((8, TOK, ROWS), F32),
-        ((8, 8, ROWS), F32), ((8, 8, ROWS), F32),
+        ((8, 8, ROWS), F32), ((8, 8, ROWS), F32), ((NX, DL, ROWS), F32), ((NX, 8, ROWS), F32),
         ((8 * TOK, ROWS), BF16), ((8 * TOK, ROWS), BF16), ((DL, ROWS), BF16), ((DL, ROWS), BF16),
         ((4, CH, 128), BF16), ((4, CH, 128), BF16), ((4, CH, 128), F32), ((4, CHA, 128), BF16),
         ((CHA, 128), F32),

time: 58.8 us -> 56.6 us (0.963)
  Pallas kernels: 58.1 us -> 55.8 us
    pallas_call x1, Pallas kernels: 57 us -> 54.7 us  [on_device(): pl.pallas_call(kernel, out_shape=[pltpu.VMEM(s, t) for s, t in outs], in_...]
where the time goes in v6:
time: 56.6 us; the launch traced here: 56.5 us
  Pallas kernels  55.8 us (99%)
  between operations  0.64 us (1%)
    pallas_call x1, Pallas kernels, on_device(): pl.pallas_call(kernel, out_shape=[pltpu.VMEM(s, t) for s, t in outs], in_...  54.7 us

profile of v6, /device:TPU:1, one launch (start us, length us, event | category | flops | bytes accessed | tf_op | source)
XLA Modules:
  0.0 56.5 jit_solution(2756842385687624264)
XLA Ops:
  0.6 54.7 %mla_backward.1 = (bf16[2,192,128]{2,1,0:T(8,128)(2,1)S(1)}, bf16[2,64,192]{2,1,0:T(8,128)(2,1)S(1)}, bf16[3,512]{1,0:T(4,128)(2,1)S(1)}, bf16[3,64]{1,0:T(4,128...) custom-call(bf16[192,2,128]{2,1,0:T(2,128)(2,1)} %q_hbm.1, ...), custom_call_target="tpu_custom_call" | custom-call | tf_op jit(solution)/shard_map/mla_backward/pallas_call | solution.py:604
  55.4 1.1 %finish.1 = (bf16[192,2,128]{2,1,0:T(2,128)(2,1)}, bf16[2,64,192]{2,1,0:T(8,128)(2,1)}, bf16[3,512]{1,0:T(4,128)(2,1)}, bf16[3,64]{1,0:T(4,128)(2,1)}, f32[2,128,512]{2,1,0:T(8,128)}, /*index=5*/f32[2,128,512]{2,1,0:T(8,128)}) custom-call(bf16[2,192,128]{2,1,0:T(8,128)(2,1)S(1)} %get-tuple-element.18.gn_in, bf16[2,64,192]{2,1,0:T(8,128)(2,1)S(1)} %get-tuple-element.19.gr_in, ...), custom_call_target="tpu_custom_call" | custom-call | tf_op jit(solution)/shard_map/finish/pallas_call | solution.py:633

commit v7 on v6

--- a/solution.py
+++ b/solution.py
@@ -375,17 +375,22 @@
         got(n, other)
         total[...] = (buf[yl].astype(F32) + other[...].astype(F32)).astype(BF16)
 
-    def peers():
-        for n, (dx, dy) in enumerate(((1, 0), (3, 0), (0, 1), (2, 0), (1, 1), (3, 1), (2, 1))):
-            yield n, (x + dx) % NX, (x + NX - dx) % NX, (yl + dy) % 2
+    def along_x(n, fin, side):
+        for d in range(1, NX):
+            send(n + d, fin.at[side, x], fin.at[side, x], device(x_=(x + d) % NX))
 
     def spread(n, fin):
-        for i, to_x, _, side in peers():
-            send(n + i, fin.at[yl, x], fin.at[yl, x], device(x_=to_x, yl_=side))
+        send(n, fin.at[yl, x], fin.at[yl, x], to_y)
+        along_x(n, fin, yl)
+
+    def relay(n, fin):
+        got(n, fin.at[1 - yl, x])
+        along_x(n + 3, fin, 1 - yl)
 
     def spread_got(n, fin):
-        for i, _, from_x, side in peers():
-            got(n + i, fin.at[side, from_x])
+        for d in range(1, NX):
+            got(n + d, fin.at[yl, (x + NX - d) % NX])
+            got(n + 3 + d, fin.at[1 - yl, (x + NX - d) % NX])
 
     for b in range(8):
         w = st[b] * (mb[b] * inv)[:1]
@@ -495,6 +500,8 @@
     spread(87, vfin)
     ring_last(81, ks, halves, k_dst, kfin)
     spread(94, kfin)
+    relay(87, vfin)
+    relay(94, kfin)
 
     out_row, in_row = iota((128, 128), 0), iota((128, 128), 1)
     owner, place = out_row // 16, out_row % 16

time: 56.6 us -> 56.3 us (level)
  no operation moved by 1% of the time
where the time goes in v7:
time: 56.3 us; the launch traced here: 56.2 us
  Pallas kernels  55.6 us (99%)
  between operations  0.64 us (1%)
    pallas_call x1, Pallas kernels, on_device(): pl.pallas_call(kernel, out_shape=[pltpu.VMEM(s, t) for s, t in outs], in_...  54.5 us

profile of v7, /device:TPU:1, one launch (start us, length us, event | category | flops | bytes accessed | tf_op | source)
XLA Modules:
  0.0 56.2 jit_solution(10283918626370267511)
XLA Ops:
  0.6 54.5 %mla_backward.1 = (bf16[2,192,128]{2,1,0:T(8,128)(2,1)S(1)}, bf16[2,64,192]{2,1,0:T(8,128)(2,1)S(1)}, bf16[3,512]{1,0:T(4,128)(2,1)S(1)}, bf16[3,64]{1,0:T(4,128...) custom-call(bf16[192,2,128]{2,1,0:T(2,128)(2,1)} %q_hbm.1, ...), custom_call_target="tpu_custom_call" | custom-call | tf_op jit(solution)/shard_map/mla_backward/pallas_call | solution.py:611
  55.1 1.1 %finish.1 = (bf16[192,2,128]{2,1,0:T(2,128)(2,1)}, bf16[2,64,192]{2,1,0:T(8,128)(2,1)}, bf16[3,512]{1,0:T(4,128)(2,1)}, bf16[3,64]{1,0:T(4,128)(2,1)}, f32[2,128,512]{2,1,0:T(8,128)}, /*index=5*/f32[2,128,512]{2,1,0:T(8,128)}) custom-call(bf16[2,192,128]{2,1,0:T(8,128)(2,1)S(1)} %get-tuple-element.18.gn_in, bf16[2,64,192]{2,1,0:T(8,128)(2,1)S(1)} %get-tuple-element.19.gr_in, ...), custom_call_target="tpu_custom_call" | custom-call | tf_op jit(solution)/shard_map/finish/pallas_call | solution.py:640

commit v8 on v7

--- a/solution.py
+++ b/solution.py
@@ -113,7 +113,6 @@
         local.append(copy)
         return copy
 
-    kr_in = fetch(kr_hbm, kr_v)
     lat_in = []
     for h in range(2):
         for t in range(4):
@@ -121,6 +120,7 @@
                 lat_hbm.at[pl.ds(h * HALF, HALF), pl.ds(t * 128, 128)],
                 agb.at[0, 0, h, pl.ds(t * HALF, HALF)],
             ))
+    kr_in = fetch(kr_hbm, kr_v)
     q_in, kup_in = fetch(q_hbm, q_v), fetch(kup_hbm, kup_v)
     go_in, vup_in = fetch(go_hbm, go_v), fetch(vup_hbm, vup_v)
     qr_in, po_in = fetch(qr_hbm, qr_v), fetch(po_hbm, po_v)
@@ -274,10 +274,9 @@
             gather_x(3, 1, p, block(k, 1, p))
         gather_sib(k, 1, p)
 
-    def on_far(j):
-        for p in range(2):
-            from_x(3, j, p)
-            gather_sib(3, j, p)
+    def on_far(j, p):
+        from_x(3, j, p)
+        gather_sib(3, j, p)
 
     heard(0)
     tell(1)
@@ -297,7 +296,8 @@
     on_from_y(1, 0)
     on_from_y(2, 1)
     turn(0)
-    on_far(0)
+    on_far(0, 0)
+    on_far(0, 1)
     from_sib(1, 0)
     attend(1, 0)
     on_from_y(1, 1)
@@ -306,9 +306,10 @@
     attend(2, 0)
     from_sib(3, 0)
     attend(3, 0)
-    on_far(1)
+    on_far(1, 0)
     from_sib(1, 1)
     attend(1, 1)
+    on_far(1, 1)
     turn(1)
     from_sib(2, 1)
     attend(2, 1)
@@ -572,15 +573,29 @@
                 to_owner(d, e).wait_send()
 
 
-def finish(gn_in, gr_in, ol_in, or_in, kfin, vfin, gn_ref, gr_ref, ol_ref, or_ref, gk_ref, gv_ref):
-    gr_ref[...] = gr_in[...]
-    ol_ref[...] = ol_in[...]
-    or_ref[...] = or_in[...]
-    for a in range(8):
+def finish(
+    gn_in, gr_in, ol_in, or_in, kfin, vfin, gn_out, gr_out, ol_out, or_out, gk_out, gv_out,
+    gn_s, gk_s, gv_s, sems,
+):
+    copies = []
+
+    def put(src, dst):
+        copy = pltpu.make_async_copy(src, dst, sems.at[len(copies)])
+        copy.start()
+        copies.append(copy)
+
+    for fin, rows, out in ((kfin, gk_s, gk_out), (vfin, gv_s, gv_out)):
         for h in range(2):
-            gk_ref[h, pl.ds(16 * a, 16), :] = kfin[a // 4, a % 4, pl.ds(16 * h, 16), :].astype(F32)
-            gv_ref[h, pl.ds(16 * a, 16), :] = vfin[a // 4, a % 4, pl.ds(16 * h, 16), :].astype(F32)
-    gn_ref[...] = jnp.stack([gn_in[0].astype(F32), gn_in[1].astype(F32)], axis=1).astype(BF16)
+            for a in range(8):
+                rows[h, pl.ds(16 * a, 16), :] = fin[a // 4, a % 4, pl.ds(16 * h, 16), :].astype(F32)
+            put(rows.at[h], out.at[h])
+    put(gr_in, gr_out)
+    put(ol_in, ol_out)
+    put(or_in, or_out)
+    gn_s[...] = jnp.stack([gn_in[0].astype(F32), gn_in[1].astype(F32)], axis=1).astype(BF16)
+    put(gn_s, gn_out)
+    for copy in copies:
+        copy.wait()
 
 
 def on_device(query_nope, query_rope, grad_output, latents, key_rope, key_up, value_up, pair_order):
@@ -641,7 +656,13 @@
         finish,
         out_shape=[jax.ShapeDtypeStruct(s, t) for s, t in results],
         in_specs=[vmem_spec] * 6,
-        out_specs=[vmem_spec] * 6,
+        out_specs=[any_spec] * 6,
+        scratch_shapes=[
+            pltpu.VMEM((TOK, 2, DN), BF16),
+            pltpu.VMEM((2, DN, DL), F32),
+            pltpu.VMEM((2, DN, DL), F32),
+            pltpu.SemaphoreType.DMA((8,)),
+        ],
         name="finish",
     )(*[pltpu.with_memory_space_constraint(r, pltpu.VMEM) for r in raw])
     return grad_nope, jnp.transpose(grad_rope, (2, 0, 1)), own_lat, own_rope, grad_kup, grad_vup

time: 56.3 us -> 56.3 us (level)
  no operation moved by 1% of the time
where the time goes in v8:
time: 56.3 us; the launch traced here: 56.1 us
  Pallas kernels  55.5 us (99%)
  between operations  0.64 us (1%)
    pallas_call x1, Pallas kernels, on_device(): pl.pallas_call(kernel, out_shape=[pltpu.VMEM(s, t) for s, t in outs], in_...  54.4 us

profile of v8, /device:TPU:1, one launch (start us, length us, event | category | flops | bytes accessed | tf_op | source)
XLA Modules:
  0.0 56.1 jit_solution(9126108338793446853)
XLA Ops:
  0.6 54.4 %mla_backward.1 = (bf16[2,192,128]{2,1,0:T(8,128)(2,1)S(1)}, bf16[2,64,192]{2,1,0:T(8,128)(2,1)S(1)}, bf16[3,512]{1,0:T(4,128)(2,1)S(1)}, bf16[3,64]{1,0:T(4,128...) custom-call(bf16[192,2,128]{2,1,0:T(2,128)(2,1)} %q_hbm.1, ...), custom_call_target="tpu_custom_call" | custom-call | tf_op jit(solution)/shard_map/mla_backward/pallas_call | solution.py:626
  55.0 1.1 %finish.1 = (bf16[192,2,128]{2,1,0:T(2,128)(2,1)}, bf16[2,64,192]{2,1,0:T(8,128)(2,1)}, bf16[3,512]{1,0:T(4,128)(2,1)}, bf16[3,64]{1,0:T(4,128)(2,1)}, f32[2,128,512]{2,1,0:T(8,128)}, /*index=5*/f32[2,128,512]{2,1,0:T(8,128)}) custom-call(bf16[2,192,128]{2,1,0:T(8,128)(2,1)S(1)} %get-tuple-element.18.gn_in, bf16[2,64,192]{2,1,0:T(8,128)(2,1)S(1)} %get-tuple-element.19.gr_in, ...), custom_call_target="tpu_custom_call" | custom-call | tf_op jit(solution)/shard_map/finish/pallas_call | solution.py:655

commit v9 on v8

--- a/solution.py
+++ b/solution.py
@@ -468,8 +468,6 @@
     gn_ref[0] = grad_nope[:TOK, :DN].astype(BF16)
     gn_ref[1] = grad_nope[TOK:, DN:].astype(BF16)
 
-    from_pair(80, kb, kry, ks)
-    ring_first(81, ks, halves, k_dst)
 
     got(54, ra1)
     got(55, rb1)
@@ -486,6 +484,8 @@
         far = (z + d) % NZ
         send(57 + d, zs.at[far], zrecv.at[d], device(z_=far))
 
+    from_pair(80, kb, kry, ks)
+    ring_first(81, ks, halves, k_dst)
     ring_second(74, vs, halves, v_dst, vkeep)
     ring_second(81, ks, halves, k_dst, kkeep)
 
@@ -502,7 +502,6 @@
     ring_last(81, ks, halves, k_dst, kfin)
     spread(94, kfin)
     relay(87, vfin)
-    relay(94, kfin)
 
     out_row, in_row = iota((128, 128), 0), iota((128, 128), 1)
     owner, place = out_row // 16, out_row % 16
@@ -542,6 +541,7 @@
             else:
                 to_owner(d, e).start()
 
+    relay(94, kfin)
     spread_got(87, vfin)
     spread_got(94, kfin)
 

time: 56.3 us -> 56.2 us (level)
  no operation moved by 1% of the time
where the time goes in v9:
time: 56.2 us; the launch traced here: 56.1 us
  Pallas kernels  55.4 us (99%)
  between operations  0.64 us (1%)
    pallas_call x1, Pallas kernels, on_device(): pl.pallas_call(kernel, out_shape=[pltpu.VMEM(s, t) for s, t in outs], in_...  54.3 us

profile of v9, /device:TPU:1, one launch (start us, length us, event | category | flops | bytes accessed | tf_op | source)
XLA Modules:
  0.0 56.1 jit_solution(6957847543598037497)
XLA Ops:
  0.6 54.3 %mla_backward.1 = (bf16[2,192,128]{2,1,0:T(8,128)(2,1)S(1)}, bf16[2,64,192]{2,1,0:T(8,128)(2,1)S(1)}, bf16[3,512]{1,0:T(4,128)(2,1)S(1)}, bf16[3,64]{1,0:T(4,128...) custom-call(bf16[192,2,128]{2,1,0:T(2,128)(2,1)} %q_hbm.1, ...), custom_call_target="tpu_custom_call" | custom-call | tf_op jit(solution)/shard_map/mla_backward/pallas_call | solution.py:626
  55.0 1.1 %finish.1 = (bf16[192,2,128]{2,1,0:T(2,128)(2,1)}, bf16[2,64,192]{2,1,0:T(8,128)(2,1)}, bf16[3,512]{1,0:T(4,128)(2,1)}, bf16[3,64]{1,0:T(4,128)(2,1)}, f32[2,128,512]{2,1,0:T(8,128)}, /*index=5*/f32[2,128,512]{2,1,0:T(8,128)}) custom-call(bf16[2,192,128]{2,1,0:T(8,128)(2,1)S(1)} %get-tuple-element.18.gn_in, bf16[2,64,192]{2,1,0:T(8,128)(2,1)S(1)} %get-tuple-element.19.gr_in, ...), custom_call_target="tpu_custom_call" | custom-call | tf_op jit(solution)/shard_map/finish/pallas_call | solution.py:655
